TPU v7x, 32 devices: a whole 2x2x4 slice. The times are simulated.
32 devices in a mesh: dp: 4 (over y, core), tower: 8 (over z, x).
Axes of the slice: x: 2, y: 2, z: 4, core: 2. Of those that a mesh axis runs over, the one named last changes fastest.
Arguments:
- attn_out: bfloat16 [4096, 4096], P(('dp', 'tower')), may hold values from -0.375 to 0.375
- out_cot: bfloat16 [4096, 4096], P(('dp', 'tower')), may hold values from -6 to 6
- modality: int32 [4096], P(('dp', 'tower')), may hold values from 0 to 2, as said below
- group_modality: int32 [8], replicated, may hold values from 0 to 2, as said below
- o_weight: bfloat16 [32768, 4096], P('tower'), as said below
Outputs:
- attn_grad: bfloat16 [4096, 4096], P(('dp', 'tower'))
- weight_grad: bfloat16 [32768, 4096], P('tower', 'dp')
Inputs may be any that keep to these rules, and one draw needn't show every extreme that they name: `group_modality`: every modality is served by at least one group. In each block of 128 tokens (one device's tokens), a modality served by k groups appears at most k * 24 times; in every block the modality served by the fewest groups (the lowest such id on a tie) appears exactly that often. `o_weight`: groups that serve the same modality hold equal rows.
All inputs are finite; a program needn't handle non-finite values.
Results may differ from a plain program's by a relative error of at most 0.014.
Values may be sent and summed in bfloat16 or wider, within the bound.
No kernel may reach another device: no remote copies, remote signals or barrier semaphores. Data moves between devices by JAX's collectives and lax.ppermute only.
A program may use at most 128 MiB of HBM per device.

v0:
```python
import functools

import jax
import jax.numpy as jnp
from jax import lax
from jax.experimental import pallas as pl
from jax.experimental.pallas import tpu as pltpu
from jax.sharding import PartitionSpec as P


NGROUP = 8
KINDS = 3
CAP = 24
BF16 = jnp.bfloat16
F32 = jnp.float32
I32 = jnp.int32


MIB = 1 << 20


def grant(mib):
    return pltpu.CompilerParams(vmem_limit_bytes=mib * MIB)


def cost(flops, moved):
    return pl.CostEstimate(flops=flops, bytes_accessed=moved, transcendentals=0)


RING = NGROUP // 2
STEPS = (0, 1, 3, 2)


def block_to(group, tower_idx):
    steps = (group // 2 - jnp.right_shift(tower_idx, 1)) & (RING - 1)
    place = jnp.int32(0)
    for at, step in enumerate(STEPS):
        place = jnp.where(steps == step, at, place)
    return place * 2 + ((group & 1) ^ (tower_idx & 1))


def target_of(tower_idx, block):
    return (tower_idx // 2 + STEPS[block // 2]) % RING * 2 + (tower_idx + block) % 2


def dispatch_matrix(tower_idx, kinds_ref, modal_row):
    tokens = modal_row.shape[1]
    earlier = lax.broadcasted_iota(I32, (tokens, tokens), 0) < lax.broadcasted_iota(
        I32, (tokens, tokens), 1
    )
    kind_rows = lax.broadcasted_iota(I32, (8, tokens), 0)
    member = jnp.where(kind_rows == modal_row, 1.0, 0.0)
    before = jnp.dot(
        member.astype(BF16),
        jnp.where(earlier, 1.0, 0.0).astype(BF16),
        preferred_element_type=F32,
    )
    order_in = jnp.sum(member * before, axis=0, keepdims=True)
    kinds = [kinds_ref[g] for g in range(NGROUP)]
    seen = [jnp.int32(0)] * KINDS
    ranks = []
    for g in range(NGROUP):
        rank = jnp.int32(0)
        for m in range(KINDS):
            hit = kinds[g] == m
            rank = jnp.where(hit, seen[m], rank)
            seen[m] = seen[m] + jnp.where(hit, 1, 0)
        ranks.append(rank)
    how_many = jnp.zeros((1, tokens), F32)
    for m in range(KINDS):
        how_many = jnp.where(modal_row == m, seen[m].astype(F32), how_many)
    inverse = 1.0 / jnp.maximum(how_many, 1.0)
    slot_idx = jnp.floor((order_in + 0.5) * inverse)
    shifted = order_in + tower_idx.astype(F32)
    target = shifted - how_many * jnp.floor((shifted + 0.5) * inverse)
    target = target.astype(I32)
    block = jnp.zeros((1, tokens), I32)
    for g in range(NGROUP):
        chosen = (modal_row == kinds[g]) & (target == ranks[g])
        block = jnp.where(chosen, block_to(g, tower_idx), block)
    place = block * CAP + slot_idx.astype(I32)
    slots = lax.broadcasted_iota(I32, (NGROUP * CAP, tokens), 0)
    return jnp.where(slots == place, 1.0, 0.0).astype(BF16)


def first_dispatch_kernel(chunks, tower_ref, kinds_hbm, modal_hbm, rows_hbm, one_hot_ref, *refs):
    out_refs, (kinds_ref, modal_ref, rows_ref, known, arrived) = refs[:NGROUP], refs[NGROUP:]
    width = rows_ref.shape[1] // chunks
    tables = [
        pltpu.make_async_copy(kinds_hbm, kinds_ref, known.at[0]),
        pltpu.make_async_copy(modal_hbm, modal_ref, known.at[1]),
    ]
    for table in tables:
        table.start()
    copies = []
    for c in range(chunks):
        columns = pl.ds(c * width, width)
        copies.append(
            pltpu.make_async_copy(rows_hbm.at[:, columns], rows_ref.at[:, columns], arrived.at[c])
        )
        copies[c].start()
    for table in tables:
        table.wait()
    one_hot_ref[...] = dispatch_matrix(tower_ref[0], kinds_ref, modal_ref[...])
    for c in range(chunks):
        columns = pl.ds(c * width, width)
        copies[c].wait()
        placed = jnp.dot(one_hot_ref[...], rows_ref[:, columns], preferred_element_type=F32)
        for k, out_ref in enumerate(out_refs):
            out_ref[:, columns] = placed[k * CAP : (k + 1) * CAP, :].astype(BF16)


def dispatch_kernel(one_hot_ref, rows_ref, *out_refs):
    placed = jnp.dot(one_hot_ref[...], rows_ref[...], preferred_element_type=F32)
    for k, out_ref in enumerate(out_refs):
        out_ref[...] = placed[k * CAP : (k + 1) * CAP, :].astype(BF16)


def dispatch_first(tower_idx, kinds, modal_row, rows):
    tokens, width = rows.shape
    chunks = 4
    slots = NGROUP * CAP
    in_smem = pl.BlockSpec(memory_space=pltpu.SMEM)
    in_vmem = pl.BlockSpec(memory_space=pltpu.VMEM)
    out = pl.pallas_call(
        functools.partial(first_dispatch_kernel, chunks),
        in_specs=[in_smem] + [pl.BlockSpec(memory_space=pltpu.HBM)] * 3,
        out_specs=[in_vmem] * (NGROUP + 1),
        out_shape=[jax.ShapeDtypeStruct((slots, tokens), BF16)]
        + [jax.ShapeDtypeStruct((CAP, width), BF16)] * NGROUP,
        scratch_shapes=[
            pltpu.SMEM((NGROUP,), I32),
            pltpu.VMEM((1, tokens), I32),
            pltpu.VMEM((tokens, width), BF16),
            pltpu.SemaphoreType.DMA((2,)),
            pltpu.SemaphoreType.DMA((chunks,)),
        ],
        cost_estimate=cost(2 * slots * tokens * width, 2 * (tokens + slots) * width),
        compiler_params=grant(56),
        name="dispatch_cot",
    )(tower_idx, kinds, modal_row, rows)
    return out[0], list(out[1:])


def dispatch_next(one_hot, rows):
    tokens, width = rows.shape
    block = min(1024, width)
    slots = one_hot.shape[0]
    return list(
        pl.pallas_call(
            dispatch_kernel,
            grid=(width // block,),
            in_specs=[
                pl.BlockSpec((slots, tokens), lambda i: (0, 0)),
                pl.BlockSpec((tokens, block), lambda i: (0, i)),
            ],
            out_specs=[pl.BlockSpec((CAP, block), lambda i: (0, i))] * NGROUP,
            out_shape=[jax.ShapeDtypeStruct((CAP, width), BF16)] * NGROUP,
            cost_estimate=cost(2 * slots * tokens * width, 2 * (tokens + slots) * width),
            compiler_params=grant(12),
            name="dispatch_attn",
        )(one_hot, rows)
    )


def pieces_kernel(count, dp_ref, *refs):
    block_refs, out_refs = refs[:count], refs[count:]
    columns = out_refs[0].shape[1]
    for f, out_ref in enumerate(out_refs):
        first = pl.multiple_of(jnp.bitwise_xor(dp_ref[0], jnp.int32(f)) * columns, 128)
        for k, block_ref in enumerate(block_refs):
            out_ref[k * CAP : (k + 1) * CAP, :] = block_ref[:, pl.ds(first, columns)]


def column_pieces(dp_idx, blocks):
    pieces = lax.axis_size("dp")
    width = blocks[0].shape[1]
    rows = len(blocks) * CAP
    whole = pl.BlockSpec(memory_space=pltpu.VMEM)
    return pl.pallas_call(
        functools.partial(pieces_kernel, len(blocks)),
        in_specs=[pl.BlockSpec(memory_space=pltpu.SMEM)] + [whole] * len(blocks),
        out_specs=[whole] * pieces,
        out_shape=[jax.ShapeDtypeStruct((rows, width // pieces), BF16)] * pieces,
        cost_estimate=cost(0, 4 * rows * width),
        compiler_params=grant(8),
        name="column_pieces",
    )(dp_idx, *blocks)


def token_grad_kernel(pieces, parts, dp_ref, *refs):
    cot_refs, weight_refs = refs[: pieces * parts], refs[pieces * parts : pieces * (parts + 1)]
    out_refs, rows_refs = refs[pieces * (parts + 1) : -pieces], refs[-pieces:]

    @pl.when(pl.program_id(0) == 0)
    def _():
        for f, rows_ref in enumerate(rows_refs):
            at = 0
            for cot_ref in cot_refs[f::pieces]:
                rows_ref[at : at + cot_ref.shape[0], :] = cot_ref[...]
                at += cot_ref.shape[0]

    grads = None
    for rows_ref, weight_ref in zip(rows_refs, weight_refs):
        term = lax.dot_general(
            rows_ref[...], weight_ref[...], (((1,), (1,)), ((), ())), preferred_element_type=F32
        )
        grads = term if grads is None else grads + term
    for k, out_ref in enumerate(out_refs):
        out_ref[...] = grads[k * CAP : (k + 1) * CAP, :].astype(BF16)


def token_grad(dp_idx, cot_pieces, weight):
    features, width = weight.shape
    pieces = len(cot_pieces[0])
    columns = width // pieces
    slots = NGROUP * CAP
    block = min(512, features)

    def weight_spec(f):
        return pl.BlockSpec((block, columns), lambda i, dp_ref: (i, jnp.bitwise_xor(dp_ref[0], f)))

    flat = [piece for part in cot_pieces for piece in part]
    return list(
        pl.pallas_call(
            functools.partial(token_grad_kernel, pieces, len(cot_pieces)),
            grid_spec=pltpu.PrefetchScalarGridSpec(
                num_scalar_prefetch=1,
                grid=(features // block,),
                in_specs=[pl.BlockSpec(piece.shape, lambda i, dp_ref: (0, 0)) for piece in flat]
                + [weight_spec(f) for f in range(pieces)],
                out_specs=[pl.BlockSpec((CAP, block), lambda i, dp_ref: (0, i))] * NGROUP,
                scratch_shapes=[pltpu.VMEM((slots, columns), BF16)] * pieces,
            ),
            out_shape=[jax.ShapeDtypeStruct((CAP, features), BF16)] * NGROUP,
            cost_estimate=cost(
                2 * slots * features * width, 2 * (features * width + 2 * slots * width)
            ),
            compiler_params=grant(24),
            name="token_grad",
        )(dp_idx, *flat, *[weight] * pieces)
    )


def rows_back(one_hot_ref, first, got_refs, rows_ref, columns):
    for k, got_ref in enumerate(got_refs):
        rows_ref[k * CAP : (k + 1) * CAP, columns] = got_ref[:, columns]
    return lax.dot_general(
        one_hot_ref[first * CAP : (first + len(got_refs)) * CAP, :],
        rows_ref[:, columns],
        (((0,), (0,)), ((), ())),
        preferred_element_type=F32,
    )


def combine_first_kernel(chunks, one_hot_ref, *refs):
    got_refs, out_ref, rows_ref = refs[:-2], refs[-2], refs[-1]
    width = out_ref.shape[1] // chunks
    for c in range(chunks):
        columns = pl.ds(c * width, width)
        out_ref[:, columns] = rows_back(one_hot_ref, 0, got_refs, rows_ref, columns).astype(BF16)


def combine_last_kernel(chunks, first, one_hot_ref, partial_ref, *refs):
    got_refs, out_hbm, rows_ref, out_ref, written = refs[:-4], *refs[-4:]
    width = out_ref.shape[1] // chunks
    copies = []
    for c in range(chunks):
        columns = pl.ds(c * width, width)
        total = rows_back(one_hot_ref, first, got_refs, rows_ref, columns)
        out_ref[:, columns] = (total + partial_ref[:, columns].astype(F32)).astype(BF16)
        copies.append(
            pltpu.make_async_copy(out_ref.at[:, columns], out_hbm.at[:, columns], written.at[c])
        )
        copies[c].start()
    for copy in copies:
        copy.wait()


def combine_first(one_hot, blocks):
    tokens = one_hot.shape[1]
    width = blocks[0].shape[1]
    rows = len(blocks) * CAP
    whole = pl.BlockSpec(memory_space=pltpu.VMEM)
    return pl.pallas_call(
        functools.partial(combine_first_kernel, 4),
        in_specs=[whole] * (1 + len(blocks)),
        out_specs=whole,
        out_shape=jax.ShapeDtypeStruct((tokens, width), BF16),
        scratch_shapes=[pltpu.VMEM((rows, width), BF16)],
        cost_estimate=cost(2 * rows * tokens * width, 2 * (tokens + rows) * width),
        compiler_params=grant(12),
        name="combine_first",
    )(one_hot, *blocks)


def combine_last(one_hot, partial, blocks):
    tokens, width = partial.shape
    chunks = 4
    rows = len(blocks) * CAP
    whole = pl.BlockSpec(memory_space=pltpu.VMEM)
    return pl.pallas_call(
        functools.partial(combine_last_kernel, chunks, NGROUP - len(blocks)),
        in_specs=[whole] * (2 + len(blocks)),
        out_specs=pl.BlockSpec(memory_space=pl.ANY),
        out_shape=jax.ShapeDtypeStruct((tokens, width), BF16),
        scratch_shapes=[
            pltpu.VMEM((rows, width), BF16),
            pltpu.VMEM((tokens, width), BF16),
            pltpu.SemaphoreType.DMA((chunks,)),
        ],
        cost_estimate=cost(2 * rows * tokens * width, 2 * (2 * tokens + rows) * width),
        compiler_params=grant(12),
        name="combine_last",
    )(one_hot, partial, *blocks)


def join_kernel(*refs):
    at = 0
    for ref in refs[:-1]:
        rows = ref.shape[0]
        refs[-1][at : at + rows, :] = ref[...]
        at += rows


def join_rows(blocks):
    if len(blocks) == 1:
        return blocks[0]
    rows = sum(block.shape[0] for block in blocks)
    width = blocks[0].shape[1]
    whole = pl.BlockSpec(memory_space=pltpu.VMEM)
    return pl.pallas_call(
        join_kernel,
        in_specs=[whole] * len(blocks),
        out_specs=whole,
        out_shape=jax.ShapeDtypeStruct((rows, width), BF16),
        cost_estimate=cost(0, 4 * rows * width),
        compiler_params=grant(8),
        name="join_rows",
    )(*blocks)


def weight_grad_kernel(n_attn, n_cot, *refs):
    attn_refs, cot_refs = refs[:n_attn], refs[n_attn : n_attn + n_cot]
    out_ref, attn_rows_ref, cot_rows_ref = refs[n_attn + n_cot :]

    @pl.when(pl.program_id(0) == 0)
    def _():
        at = 0
        for cot_ref in cot_refs:
            rows = cot_ref.shape[0]
            cot_rows_ref[at : at + rows, :] = cot_ref[...]
            at += rows

    at = 0
    for attn_ref in attn_refs:
        rows = attn_ref.shape[0]
        attn_rows_ref[at : at + rows, :] = attn_ref[...]
        at += rows
    out_ref[...] = lax.dot_general(
        attn_rows_ref[...],
        cot_rows_ref[...],
        (((0,), (0,)), ((), ())),
        preferred_element_type=F32,
    ).astype(out_ref.dtype)


def weight_grad_of(attn_parts, cot_parts):
    features = attn_parts[0].shape[1]
    columns = cot_parts[0].shape[1]
    rows = sum(part.shape[0] for part in attn_parts)
    block = min(512, features)
    return pl.pallas_call(
        functools.partial(weight_grad_kernel, len(attn_parts), len(cot_parts)),
        grid=(features // block,),
        in_specs=[pl.BlockSpec((part.shape[0], block), lambda i: (0, i)) for part in attn_parts]
        + [pl.BlockSpec((part.shape[0], columns), lambda i: (0, 0)) for part in cot_parts],
        out_specs=pl.BlockSpec((block, columns), lambda i: (i, 0)),
        out_shape=jax.ShapeDtypeStruct((features, columns), BF16),
        scratch_shapes=[pltpu.VMEM((rows, block), BF16), pltpu.VMEM((rows, columns), BF16)],
        cost_estimate=cost(
            2 * rows * features * columns, 2 * (rows * (features + columns) + features * columns)
        ),
        compiler_params=grant(20),
        name="weight_grad",
    )(*attn_parts, *cot_parts)


def flip_over(axis, value, flip):
    size = lax.axis_size(axis)
    return lax.ppermute(value, axis, [(i, i ^ flip) for i in range(size)])


def swap_blocks(blocks, back=False):
    got = [blocks[0]]
    for k in range(1, NGROUP):
        pairs = [(t, target_of(t, k)) for t in range(NGROUP)]
        if back:
            pairs = [(target, source) for source, target in pairs]
        got.append(lax.ppermute(blocks[k], "tower", pairs))
    return got


def gather_flips(value):
    parts = {0: value}
    flip = lax.axis_size("dp") // 2
    while flip:
        for known in list(parts):
            parts[known ^ flip] = flip_over("dp", parts[known], flip)
        flip //= 2
    return parts


COT_PARTS = {"cot_early": (0, 1, 2, 3), "cot_late": (4, 5, 6, 7)}
ATTN_PARTS = {"attn_a": (0, 1), "attn_b": (2,), "attn_c": (3, 4, 5), "attn_d": (6, 7)}
LAST = (6, 7)


def small_towers(attn_out, out_cot, modality, group_modality, o_weight):
    tower_idx = lax.axis_index("tower").astype(I32)
    dp_idx = lax.axis_index("dp").astype(I32).reshape(1)
    dp_count = lax.axis_size("dp")

    one_hot, cot_blocks = dispatch_first(
        tower_idx.reshape(1), group_modality, modality.reshape(1, -1), out_cot
    )
    attn_blocks = dispatch_next(one_hot, attn_out)
    cot_got = swap_blocks(cot_blocks)
    attn_got = swap_blocks(attn_blocks)
    cot_pieces, cot_moved = [], []
    for blocks in COT_PARTS.values():
        pieces = column_pieces(dp_idx, [cot_got[k] for k in blocks])
        cot_pieces.append(pieces)
        cot_moved.append(
            [flip_over("dp", piece, flip) if flip else piece for flip, piece in enumerate(pieces)]
        )
    cot_parts = [moved[flip] for flip in range(dp_count) for moved in cot_moved]
    grads = token_grad(dp_idx, cot_pieces, o_weight)
    returned = swap_blocks(grads, back=True)
    partial = combine_first(one_hot, [returned[k] for k in range(NGROUP) if k not in LAST])
    attn_grad = combine_last(one_hot, partial, [returned[k] for k in LAST])

    parts = []
    for blocks in ATTN_PARTS.values():
        joined = join_rows([attn_got[k] for k in blocks])
        parts.append(gather_flips(joined))
    attn_parts = [part[flip] for flip in range(dp_count) for part in parts]
    return attn_grad, weight_grad_of(attn_parts, cot_parts)


def large_towers(attn_out, out_cot, modality, group_modality, o_weight):
    tower_idx = lax.axis_index("tower").astype(I32)
    tower_count = lax.axis_size("tower")
    dp_idx = lax.axis_index("dp")
    dp_count = lax.axis_size("dp")
    group_size = tower_count // NGROUP
    piece_rows, width = o_weight.shape
    tokens = attn_out.shape[0]
    piece_cols = width // dp_count
    modal_row = modality.reshape(1, tokens)
    group_ids = jnp.arange(NGROUP, dtype=I32)
    member = modal_row == jnp.arange(KINDS, dtype=I32)[:, None]
    before = jnp.cumsum(member.astype(I32), axis=1) - 1
    order_in = jnp.sum(jnp.where(member, before, 0), axis=0)
    group_of = (group_modality[:, None] == jnp.arange(KINDS, dtype=I32)[None, :]).astype(I32)
    group_rank = jnp.sum((jnp.cumsum(group_of, axis=0) - group_of) * group_of, axis=1)
    how_many = jnp.sum(member * jnp.sum(group_of, axis=0)[:, None], axis=0)
    target = (order_in + tower_idx) % how_many
    chosen = (group_modality[:, None] == modal_row) & (group_rank[:, None] == target[None, :])
    routed = jnp.sum(chosen.astype(I32) * group_ids[:, None], axis=0)
    place = routed * CAP + order_in // how_many
    one_hot = (place[None, :] == jnp.arange(NGROUP * CAP, dtype=I32)[:, None]).astype(BF16)

    def swap(value):
        return lax.all_to_all(value, "tower", split_axis=0, concat_axis=0, tiled=True)

    cot_group = jnp.dot(one_hot, out_cot, preferred_element_type=F32).astype(BF16)
    attn_group = jnp.dot(one_hot, attn_out, preferred_element_type=F32).astype(BF16)
    cot_send = jnp.broadcast_to(
        cot_group.reshape(NGROUP, 1, CAP, width), (NGROUP, group_size, CAP, width)
    ).reshape(tower_count, CAP, width)
    attn_send = (
        attn_group.reshape(NGROUP, CAP, group_size, piece_rows)
        .transpose(0, 2, 1, 3)
        .reshape(tower_count, CAP, piece_rows)
    )
    cot_rows = swap(cot_send).reshape(tower_count * CAP, width)
    attn_rows = swap(attn_send).reshape(tower_count * CAP, piece_rows)
    grads = lax.dot_general(
        cot_rows, o_weight, (((1,), (1,)), ((), ())), preferred_element_type=F32
    ).astype(BF16)
    returned = (
        swap(grads.reshape(tower_count, CAP, piece_rows))
        .reshape(NGROUP, group_size, CAP, piece_rows)
        .transpose(0, 2, 1, 3)
        .reshape(NGROUP * CAP, width)
    )
    attn_grad = lax.dot_general(
        one_hot, returned, (((0,), (0,)), ((), ())), preferred_element_type=F32
    ).astype(BF16)
    cot_parts = []
    for flip in range(dp_count):
        part = lax.dynamic_slice_in_dim(cot_rows, (dp_idx ^ flip) * piece_cols, piece_cols, 1)
        cot_parts.append(flip_over("dp", part, flip) if flip else part)
    attn_parts = gather_flips(attn_rows)
    return attn_grad, weight_grad_of([attn_parts[flip] for flip in range(dp_count)], cot_parts)


def per_device(*args):
    if lax.axis_size("tower") == NGROUP:
        return small_towers(*args)
    return large_towers(*args)


def solution(mesh):
    return jax.shard_map(
        per_device,
        mesh=mesh,
        in_specs=(
            P(("dp", "tower"), None),
            P(("dp", "tower"), None),
            P(("dp", "tower")),
            P(),
            P("tower", None),
        ),
        out_specs=(P(("dp", "tower"), None), P("tower", "dp")),
        check_vma=False,
    )
```

profile of v0, /device:TPU:0, one launch (start us, length us, event | category | flops | bytes accessed | tf_op | source)
XLA Modules:
  0.0 161.8 jit_solution(7122574776447664874)
XLA Ops:
  0.6 3.3 %dispatch_cot.1 = (bf16[192,128]{1,0:T(8,128)(2,1)}, bf16[24,4096]{1,0:T(8,128)(2,1)}, bf16[24,4096]{1,0:T(8,128)(2,1)}, bf16[24,4096]{1,0:T(8,128)(2,1)}, bf16[...) custom-call(s32[1]{0:T(128)} %bitcast.tower_ref, ...), custom_call_target="tpu_custom_call" | custom-call | flops 201326592 | bytes 2621440 | tf_op jit(solution)/shard_map/dispatch_cot/pallas_call | solution.py:125
  3.9 3.0 %collective-permute-start = (bf16[24,4096]{1,0:T(8,128)(2,1)}, bf16[24,4096]{1,0:T(8,128)(2,1)S(1)}, u32[]{:S(2)}, u32[]{:S(2)}) collective-permute-start(bf16[24,4096]{1,0:T(8,128)(2,1)} %get-tuple-element.37), channel_id=1, source_target_pairs={{0,1},{1,0},{2,3},{3,2},{4,5},{5,4},{6,7},{7,6},{8,9},{9,8},{10,11... | collective-permute-start | bytes 589832 | tf_op jit(solution)/shard_map/ppermute | solution.py:400
  6.9 1.6 collective-permute-start.1
  8.5 1.6 collective-permute-start.2
  10.1 2.2 %collective-permute-start.3 = (bf16[24,4096]{1,0:T(8,128)(2,1)}, bf16[24,4096]{1,0:T(8,128)(2,1)S(1)}, u32[]{:S(2)}, u32[]{:S(2)}) collective-permute-start(bf16[24,4096]{1,0:T(8,128)(2,1)} %get-tuple-element.44), channel_id=1, source_target_pairs={{0,6},{1,7},{2,0},{3,1},{4,2},{5,3},{6,4},{7,5},{8,14},{9,15},{10,... | collective-permute-start | bytes 589832 | tf_op jit(solution)/shard_map/ppermute | solution.py:400
  12.3 1.4 collective-permute-start.4
  13.7 1.2 copy-done
  14.9 0.8 copy-done.1
  15.7 1.2 dispatch_attn.1
  17.0 0.0 collective-permute-done.refs_1_
  17.0 0.9 collective-permute-start.5
  17.9 0.0 collective-permute-done.1.refs_2_
  17.9 1.9 %collective-permute-start.6 = (bf16[24,4096]{1,0:T(8,128)(2,1)}, bf16[24,4096]{1,0:T(8,128)(2,1)S(1)}, u32[]{:S(2)}, u32[]{:S(2)}) collective-permute-start(bf16[24,4096]{1,0:T(8,128)(2,1)} %get-tuple-element.47), channel_id=1, source_target_pairs={{0,5},{1,4},{2,7},{3,6},{4,1},{5,0},{6,3},{7,2},{8,13},{9,12},{10,... | collective-permute-start | bytes 589832 | tf_op jit(solution)/shard_map/ppermute | solution.py:400
  19.8 1.0 collective-permute-done.2.refs_3_
  20.7 1.7 %collective-permute-start.14 = (bf16[24,4096]{1,0:T(8,128)(2,1)S(1)}, bf16[24,4096]{1,0:T(8,128)(2,1)S(1)}, u32[]{:S(2)}, u32[]{:S(2)}) collective-permute-start(bf16[24,4096]{1,0:T(8,128)(2,1)S(1)} %get-tuple-element.61), channel_id=1, source_target_pairs={{0,1},{1,0},{2,3},{3,2},{4,5},{5,4},{6,7},{7,6},{8,9},{9,8},{10,11... | collective-permute-start | bytes 589832 | tf_op jit(solution)/shard_map/ppermute | solution.py:400
  22.5 1.4 collective-permute-done.3.refs_0_
  23.9 11.9 %collective-permute-start.15 = (bf16[24,4096]{1,0:T(8,128)(2,1)S(1)}, bf16[24,4096]{1,0:T(8,128)(2,1)S(1)}, u32[]{:S(2)}, u32[]{:S(2)}) collective-permute-start(bf16[24,4096]{1,0:T(8,128)(2,1)S(1)} %get-tuple-element.62), channel_id=1, source_target_pairs={{0,2},{1,3},{2,4},{3,5},{4,6},{5,7},{6,0},{7,1},{8,10},{9,11},{10,... | collective-permute-start | bytes 589832 | tf_op jit(solution)/shard_map/ppermute | solution.py:400
  35.8 0.0 collective-permute-done.4.refs_1_
  35.8 3.8 %collective-permute-start.16 = (bf16[24,4096]{1,0:T(8,128)(2,1)S(1)}, bf16[24,4096]{1,0:T(8,128)(2,1)S(1)}, u32[]{:S(2)}, u32[]{:S(2)}) collective-permute-start(bf16[24,4096]{1,0:T(8,128)(2,1)S(1)} %get-tuple-element.63), channel_id=1, source_target_pairs={{0,3},{1,2},{2,5},{3,4},{4,7},{5,6},{6,1},{7,0},{8,11},{9,10},{10,... | collective-permute-start | bytes 589832 | tf_op jit(solution)/shard_map/ppermute | solution.py:400
  39.6 0.9 copy-done.3
  40.5 0.1 column_pieces.2
  40.6 8.6 %collective-permute-done.5.refs_2_ = bf16[24,4096]{1,0:T(8,128)(2,1)S(1)} collective-permute-done((bf16[24,4096]{1,0:T(8,128)(2,1)}, bf16[24,4096]{1,0:T(8,128)(2,1)S(1)}, u32[]{:S(2)}, u32[]{:S(2)}) %collective-permute-start.5) | collective-permute-done | bytes 196640 | tf_op jit(solution)/shard_map/ppermute | solution.py:400
  49.2 0.0 collective-permute-start.17
  49.2 4.2 %collective-permute-done.6.refs_3_ = bf16[24,4096]{1,0:T(8,128)(2,1)S(1)} collective-permute-done((bf16[24,4096]{1,0:T(8,128)(2,1)}, bf16[24,4096]{1,0:T(8,128)(2,1)S(1)}, u32[]{:S(2)}, u32[]{:S(2)}) %collective-permute-start.6) | collective-permute-done | bytes 196640 | tf_op jit(solution)/shard_map/ppermute | solution.py:400
  53.4 0.0 collective-permute-start.18
  53.4 0.0 collective-permute-done.15.refs_1_
  53.4 3.8 %collective-permute-start.20 = (bf16[24,4096]{1,0:T(8,128)(2,1)S(1)}, bf16[24,4096]{1,0:T(8,128)(2,1)S(1)}, u32[]{:S(2)}, u32[]{:S(2)}) collective-permute-start(bf16[24,4096]{1,0:T(8,128)(2,1)S(1)} %get-tuple-element.67), channel_id=1, source_target_pairs={{0,5},{1,4},{2,7},{3,6},{4,1},{5,0},{6,3},{7,2},{8,13},{9,12},{10,... | collective-permute-start | bytes 589832 | tf_op jit(solution)/shard_map/ppermute | solution.py:400
  57.2 0.1 column_pieces.3
  57.3 0.3 collective-permute-done.17.refs_1_
  57.6 1.5 collective-permute-start.35
  59.1 2.6 %collective-permute-done.18.refs_2_ = bf16[24,4096]{1,0:T(8,128)(2,1)S(1)} collective-permute-done((bf16[24,4096]{1,0:T(8,128)(2,1)S(1)}, bf16[24,4096]{1,0:T(8,128)(2,1)S(1)}, u32[]{:S(2)}, u32[]{:S(2)}) %collective-permute-start.18) | collective-permute-done | bytes 196640 | tf_op jit(solution)/shard_map/ppermute | solution.py:400
  61.7 0.9 collective-permute-start.37
  62.6 11.9 %collective-permute-done.19.refs_0_ = bf16[24,4096]{1,0:T(8,128)(2,1)S(1)} collective-permute-done((bf16[24,4096]{1,0:T(8,128)(2,1)S(1)}, bf16[24,4096]{1,0:T(8,128)(2,1)S(1)}, u32[]{:S(2)}, u32[]{:S(2)}) %collective-permute-start.19) | collective-permute-done | bytes 196640 | tf_op jit(solution)/shard_map/ppermute | solution.py:400
  74.5 4.1 %collective-permute-done.20.refs_1_ = bf16[24,4096]{1,0:T(8,128)(2,1)S(1)} collective-permute-done((bf16[24,4096]{1,0:T(8,128)(2,1)S(1)}, bf16[24,4096]{1,0:T(8,128)(2,1)S(1)}, u32[]{:S(2)}, u32[]{:S(2)}) %collective-permute-start.20) | collective-permute-done | bytes 196640 | tf_op jit(solution)/shard_map/ppermute | solution.py:400
  78.6 1.5 collective-permute-start.36
  80.1 17.3 %token_grad.1 = (bf16[24,4096]{1,0:T(8,128)(2,1)S(1)}, bf16[24,4096]{1,0:T(8,128)(2,1)S(1)}, bf16[24,4096]{1,0:T(8,128)(2,1)S(1)}, bf16[24,4096]{1,0:T(8,128)(2,...) custom-call(s32[1]{0:T(128)} %bitcast.2.dp_ref, ...), custom_call_target="tpu_custom_call" | custom-call | flops 6442450944 | bytes 36700160 | tf_op jit(solution)/shard_map/token_grad/pallas_call | solution.py:225
  97.4 0.0 collective-permute-done.35.refs_20_
  97.4 1.6 collective-permute-start.7
  99.0 1.7 %collective-permute-start.8 = (bf16[24,4096]{1,0:T(8,128)(2,1)S(1)}, bf16[24,4096]{1,0:T(8,128)(2,1)S(1)}, u32[]{:S(2)}, u32[]{:S(2)}) collective-permute-start(bf16[24,4096]{1,0:T(8,128)(2,1)S(1)} %get-tuple-element.54), channel_id=1, source_target_pairs={{2,0},{3,1},{4,2},{5,3},{6,4},{7,5},{0,6},{1,7},{10,8},{11,9},{12,... | collective-permute-start | bytes 589832 | tf_op jit(solution)/shard_map/ppermute | solution.py:400
  100.7 0.0 collective-permute-start.9
  100.7 0.0 collective-permute-done.36.refs_21_
  100.7 2.0 %collective-permute-start.10 = (bf16[24,4096]{1,0:T(8,128)(2,1)S(1)}, bf16[24,4096]{1,0:T(8,128)(2,1)S(1)}, u32[]{:S(2)}, u32[]{:S(2)}) collective-permute-start(bf16[24,4096]{1,0:T(8,128)(2,1)S(1)} %get-tuple-element.56), channel_id=1, source_target_pairs={{6,0},{7,1},{0,2},{1,3},{2,4},{3,5},{4,6},{5,7},{14,8},{15,9},{8,1... | collective-permute-start | bytes 589832 | tf_op jit(solution)/shard_map/ppermute | solution.py:400
  102.7 0.0 collective-permute-done.38.refs_23_
  102.7 1.3 collective-permute-start.11
  104.0 0.9 collective-permute-done.7.refs_1_
  104.9 1.5 collective-permute-start.27
  106.4 0.4 collective-permute-done.8.refs_2_
  106.8 0.2 collective-permute-start.12
  107.0 11.6 %collective-permute-done.9.refs_3_ = bf16[24,4096]{1,0:T(8,128)(2,1)S(1)} collective-permute-done((bf16[24,4096]{1,0:T(8,128)(2,1)S(1)}, bf16[24,4096]{1,0:T(8,128)(2,1)S(1)}, u32[]{:S(2)}, u32[]{:S(2)}) %collective-permute-start.9) | collective-permute-done | bytes 196640 | tf_op jit(solution)/shard_map/ppermute | solution.py:400
  118.6 2.6 %collective-permute-start.26 = (bf16[24,4096]{1,0:T(8,128)(2,1)S(1)}, bf16[24,4096]{1,0:T(8,128)(2,1)S(1)}, u32[]{:S(2)}, u32[]{:S(2)}) collective-permute-start(bf16[24,4096]{1,0:T(8,128)(2,1)S(1)} %collective-permute-done.15.refs_1_), channel_id=1, source_target_pairs={{0,16},{8,24},{16,0},{24,8},{1,17},{9,25},{17,1},{25,9},{2,18},{10... | collective-permute-start | bytes 589832 | tf_op jit(solution)/shard_map/ppermute | solution.py:391
  121.2 0.0 collective-permute-done.10.refs_4_
  121.2 0.1 collective-permute-start.22
  121.4 10.0 %collective-permute-done.12.refs_0_ = bf16[24,4096]{1,0:T(8,128)(2,1)S(1)} collective-permute-done((bf16[24,4096]{1,0:T(8,128)(2,1)S(1)}, bf16[24,4096]{1,0:T(8,128)(2,1)S(1)}, u32[]{:S(2)}, u32[]{:S(2)}) %collective-permute-start.12) | collective-permute-done | bytes 196640 | tf_op jit(solution)/shard_map/ppermute | solution.py:400
  131.4 1.0 collective-permute-start.28
  132.4 3.1 %collective-permute-done.13.refs_1_ = bf16[24,4096]{1,0:T(8,128)(2,1)S(1)} collective-permute-done((bf16[24,4096]{1,0:T(8,128)(2,1)S(1)}, bf16[24,4096]{1,0:T(8,128)(2,1)S(1)}, u32[]{:S(2)}, u32[]{:S(2)}) %collective-permute-start.13) | collective-permute-done | bytes 196640 | tf_op jit(solution)/shard_map/ppermute | solution.py:400
  135.5 0.6 collective-permute-start.25
  136.1 0.2 collective-permute-start.23
  136.4 0.3 collective-permute-start.31
  136.6 6.7 %collective-permute-done.28.refs_11_ = bf16[48,4096]{1,0:T(8,128)(2,1)S(1)} collective-permute-done((bf16[48,4096]{1,0:T(8,128)(2,1)S(1)}, bf16[48,4096]{1,0:T(8,128)(2,1)S(1)}, u32[]{:S(2)}, u32[]{:S(2)}) %collective-permute-start.28) | collective-permute-done | bytes 393248 | tf_op jit(solution)/shard_map/ppermute | solution.py:391
  143.4 0.5 collective-permute-start.32
  143.9 5.6 %collective-permute-done.25.refs_8_ = bf16[48,4096]{1,0:T(8,128)(2,1)S(1)} collective-permute-done((bf16[48,4096]{1,0:T(8,128)(2,1)S(1)}, bf16[48,4096]{1,0:T(8,128)(2,1)S(1)}, u32[]{:S(2)}, u32[]{:S(2)}) %collective-permute-start.25) | collective-permute-done | bytes 393248 | tf_op jit(solution)/shard_map/ppermute | solution.py:391
  149.5 0.5 combine_first.1.partial_ref
  150.0 1.3 combine_last.1
  151.3 10.5 %weight_grad.1 = bf16[4096,1024]{1,0:T(8,128)(2,1)} custom-call(bf16[48,4096]{1,0:T(8,128)(2,1)S(1)} %join_rows.3.refs_0_, bf16[24,4096]{1,0:T(8,128)(2,1)S(1)} %collective-permute-done.15.refs_1_, bf16[72,4096]{1,0:T(8,128)(2,1)S(1)} %join_rows.4.refs_2_, bf16[48,4096]{1,0:T(8,128)(2,1)S(1)} %join_rows.5.refs_3_, ...), custom_call_target="tpu_custom_call" | custom-call | flops 6442450944 | bytes 16252928 | tf_op jit(solution)/shard_map/weight_grad/pallas_call | solution.py:373
  (33 shorter events, 0.2 us)
Async XLA Ops:
  3.9 13.1 %collective-permute-start = (bf16[24,4096]{1,0:T(8,128)(2,1)}, bf16[24,4096]{1,0:T(8,128)(2,1)S(1)}, u32[]{:S(2)}, u32[]{:S(2)}) collective-permute-start(bf16[24,4096]{1,0:T(8,128)(2,1)} %get-tuple-element.37), channel_id=1, source_target_pairs={{0,1},{1,0},{2,3},{3,2},{4,5},{5,4},{6,7},{7,6},{8,9},{9,8},{10,11... | collective-permute-start | bytes 589832 | tf_op jit(solution)/shard_map/ppermute | solution.py:400
  6.9 10.9 %collective-permute-start.1 = (bf16[24,4096]{1,0:T(8,128)(2,1)}, bf16[24,4096]{1,0:T(8,128)(2,1)S(1)}, u32[]{:S(2)}, u32[]{:S(2)}) collective-permute-start(bf16[24,4096]{1,0:T(8,128)(2,1)} %get-tuple-element.38), channel_id=1, source_target_pairs={{0,2},{1,3},{2,4},{3,5},{4,6},{5,7},{6,0},{7,1},{8,10},{9,11},{10,... | collective-permute-start | bytes 589832 | tf_op jit(solution)/shard_map/ppermute | solution.py:400
  8.5 12.2 %collective-permute-start.2 = (bf16[24,4096]{1,0:T(8,128)(2,1)}, bf16[24,4096]{1,0:T(8,128)(2,1)S(1)}, u32[]{:S(2)}, u32[]{:S(2)}) collective-permute-start(bf16[24,4096]{1,0:T(8,128)(2,1)} %get-tuple-element.39), channel_id=1, source_target_pairs={{0,3},{1,2},{2,5},{3,4},{4,7},{5,6},{6,1},{7,0},{8,11},{9,10},{10,... | collective-permute-start | bytes 589832 | tf_op jit(solution)/shard_map/ppermute | solution.py:400
  10.1 13.8 %collective-permute-start.3 = (bf16[24,4096]{1,0:T(8,128)(2,1)}, bf16[24,4096]{1,0:T(8,128)(2,1)S(1)}, u32[]{:S(2)}, u32[]{:S(2)}) collective-permute-start(bf16[24,4096]{1,0:T(8,128)(2,1)} %get-tuple-element.44), channel_id=1, source_target_pairs={{0,6},{1,7},{2,0},{3,1},{4,2},{5,3},{6,4},{7,5},{8,14},{9,15},{10,... | collective-permute-start | bytes 589832 | tf_op jit(solution)/shard_map/ppermute | solution.py:400
  12.3 23.5 %collective-permute-start.4 = (bf16[24,4096]{1,0:T(8,128)(2,1)}, bf16[24,4096]{1,0:T(8,128)(2,1)S(1)}, u32[]{:S(2)}, u32[]{:S(2)}) collective-permute-start(bf16[24,4096]{1,0:T(8,128)(2,1)} %get-tuple-element.45), channel_id=1, source_target_pairs={{0,7},{1,6},{2,1},{3,0},{4,3},{5,2},{6,5},{7,4},{8,15},{9,14},{10,... | collective-permute-start | bytes 589832 | tf_op jit(solution)/shard_map/ppermute | solution.py:400
  13.7 1.2 copy-start
  14.9 0.8 copy-start.1
  17.0 32.2 %collective-permute-start.5 = (bf16[24,4096]{1,0:T(8,128)(2,1)}, bf16[24,4096]{1,0:T(8,128)(2,1)S(1)}, u32[]{:S(2)}, u32[]{:S(2)}) collective-permute-start(bf16[24,4096]{1,0:T(8,128)(2,1)} %get-tuple-element.46), channel_id=1, source_target_pairs={{0,4},{1,5},{2,6},{3,7},{4,0},{5,1},{6,2},{7,3},{8,12},{9,13},{10,... | collective-permute-start | bytes 589832 | tf_op jit(solution)/shard_map/ppermute | solution.py:400
  17.9 35.5 %collective-permute-start.6 = (bf16[24,4096]{1,0:T(8,128)(2,1)}, bf16[24,4096]{1,0:T(8,128)(2,1)S(1)}, u32[]{:S(2)}, u32[]{:S(2)}) collective-permute-start(bf16[24,4096]{1,0:T(8,128)(2,1)} %get-tuple-element.47), channel_id=1, source_target_pairs={{0,5},{1,4},{2,7},{3,6},{4,1},{5,0},{6,3},{7,2},{8,13},{9,12},{10,... | collective-permute-start | bytes 589832 | tf_op jit(solution)/shard_map/ppermute | solution.py:400
  20.7 32.6 %collective-permute-start.14 = (bf16[24,4096]{1,0:T(8,128)(2,1)S(1)}, bf16[24,4096]{1,0:T(8,128)(2,1)S(1)}, u32[]{:S(2)}, u32[]{:S(2)}) collective-permute-start(bf16[24,4096]{1,0:T(8,128)(2,1)S(1)} %get-tuple-element.61), channel_id=1, source_target_pairs={{0,1},{1,0},{2,3},{3,2},{4,5},{5,4},{6,7},{7,6},{8,9},{9,8},{10,11... | collective-permute-start | bytes 589832 | tf_op jit(solution)/shard_map/ppermute | solution.py:400
  23.9 29.5 %collective-permute-start.15 = (bf16[24,4096]{1,0:T(8,128)(2,1)S(1)}, bf16[24,4096]{1,0:T(8,128)(2,1)S(1)}, u32[]{:S(2)}, u32[]{:S(2)}) collective-permute-start(bf16[24,4096]{1,0:T(8,128)(2,1)S(1)} %get-tuple-element.62), channel_id=1, source_target_pairs={{0,2},{1,3},{2,4},{3,5},{4,6},{5,7},{6,0},{7,1},{8,10},{9,11},{10,... | collective-permute-start | bytes 589832 | tf_op jit(solution)/shard_map/ppermute | solution.py:400
  35.8 21.4 %collective-permute-start.16 = (bf16[24,4096]{1,0:T(8,128)(2,1)S(1)}, bf16[24,4096]{1,0:T(8,128)(2,1)S(1)}, u32[]{:S(2)}, u32[]{:S(2)}) collective-permute-start(bf16[24,4096]{1,0:T(8,128)(2,1)S(1)} %get-tuple-element.63), channel_id=1, source_target_pairs={{0,3},{1,2},{2,5},{3,4},{4,7},{5,6},{6,1},{7,0},{8,11},{9,10},{10,... | collective-permute-start | bytes 589832 | tf_op jit(solution)/shard_map/ppermute | solution.py:400
  39.6 0.9 copy-start.3
  49.2 8.4 %collective-permute-start.17 = (bf16[24,4096]{1,0:T(8,128)(2,1)S(1)}, bf16[24,4096]{1,0:T(8,128)(2,1)S(1)}, u32[]{:S(2)}, u32[]{:S(2)}) collective-permute-start(bf16[24,4096]{1,0:T(8,128)(2,1)S(1)} %get-tuple-element.64), channel_id=1, source_target_pairs={{0,6},{1,7},{2,0},{3,1},{4,2},{5,3},{6,4},{7,5},{8,14},{9,15},{10,... | collective-permute-start | bytes 589832 | tf_op jit(solution)/shard_map/ppermute | solution.py:400
  53.4 8.3 %collective-permute-start.18 = (bf16[24,4096]{1,0:T(8,128)(2,1)S(1)}, bf16[24,4096]{1,0:T(8,128)(2,1)S(1)}, u32[]{:S(2)}, u32[]{:S(2)}) collective-permute-start(bf16[24,4096]{1,0:T(8,128)(2,1)S(1)} %get-tuple-element.65), channel_id=1, source_target_pairs={{0,7},{1,6},{2,1},{3,0},{4,3},{5,2},{6,5},{7,4},{8,15},{9,14},{10,... | collective-permute-start | bytes 589832 | tf_op jit(solution)/shard_map/ppermute | solution.py:400
  53.4 21.1 %collective-permute-start.19 = (bf16[24,4096]{1,0:T(8,128)(2,1)S(1)}, bf16[24,4096]{1,0:T(8,128)(2,1)S(1)}, u32[]{:S(2)}, u32[]{:S(2)}) collective-permute-start(bf16[24,4096]{1,0:T(8,128)(2,1)S(1)} %get-tuple-element.66), channel_id=1, source_target_pairs={{0,4},{1,5},{2,6},{3,7},{4,0},{5,1},{6,2},{7,3},{8,12},{9,13},{10,... | collective-permute-start | bytes 589832 | tf_op jit(solution)/shard_map/ppermute | solution.py:400
  53.4 25.2 %collective-permute-start.20 = (bf16[24,4096]{1,0:T(8,128)(2,1)S(1)}, bf16[24,4096]{1,0:T(8,128)(2,1)S(1)}, u32[]{:S(2)}, u32[]{:S(2)}) collective-permute-start(bf16[24,4096]{1,0:T(8,128)(2,1)S(1)} %get-tuple-element.67), channel_id=1, source_target_pairs={{0,5},{1,4},{2,7},{3,6},{4,1},{5,0},{6,3},{7,2},{8,13},{9,12},{10,... | collective-permute-start | bytes 589832 | tf_op jit(solution)/shard_map/ppermute | solution.py:400
  57.2 22.8 %collective-permute-start.33 = (bf16[96,1024]{1,0:T(8,128)(2,1)S(1)}, bf16[96,1024]{1,0:T(8,128)(2,1)S(1)}, u32[]{:S(2)}, u32[]{:S(2)}) collective-permute-start(bf16[96,1024]{1,0:T(8,128)(2,1)S(1)} %get-tuple-element.41.refs_1_), channel_id=1, source_target_pairs={{0,8},{8,0},{16,24},{24,16},{1,9},{9,1},{17,25},{25,17},{2,10},{10... | collective-permute-start | bytes 589832 | tf_op jit(solution)/shard_map/ppermute | solution.py:391
  57.6 39.8 %collective-permute-start.35 = (bf16[96,1024]{1,0:T(8,128)(2,1)S(1)}, bf16[96,1024]{1,0:T(8,128)(2,1)S(1)}, u32[]{:S(2)}, u32[]{:S(2)}) collective-permute-start(bf16[96,1024]{1,0:T(8,128)(2,1)S(1)} %get-tuple-element.42.refs_2_), channel_id=1, source_target_pairs={{0,16},{8,24},{16,0},{24,8},{1,17},{9,25},{17,1},{25,9},{2,18},{10... | collective-permute-start | bytes 589832 | tf_op jit(solution)/shard_map/ppermute | solution.py:391
  61.7 37.3 %collective-permute-start.37 = (bf16[96,1024]{1,0:T(8,128)(2,1)S(1)}, bf16[96,1024]{1,0:T(8,128)(2,1)S(1)}, u32[]{:S(2)}, u32[]{:S(2)}) collective-permute-start(bf16[96,1024]{1,0:T(8,128)(2,1)S(1)} %get-tuple-element.43.refs_3_), channel_id=1, source_target_pairs={{0,24},{8,16},{16,8},{24,0},{1,25},{9,17},{17,9},{25,1},{2,26},{10... | collective-permute-start | bytes 589832 | tf_op jit(solution)/shard_map/ppermute | solution.py:391
  74.5 26.2 %collective-permute-start.34 = (bf16[96,1024]{1,0:T(8,128)(2,1)S(1)}, bf16[96,1024]{1,0:T(8,128)(2,1)S(1)}, u32[]{:S(2)}, u32[]{:S(2)}) collective-permute-start(bf16[96,1024]{1,0:T(8,128)(2,1)S(1)} %get-tuple-element.49.refs_5_), channel_id=1, source_target_pairs={{0,8},{8,0},{16,24},{24,16},{1,9},{9,1},{17,25},{25,17},{2,10},{10... | collective-permute-start | bytes 589832 | tf_op jit(solution)/shard_map/ppermute | solution.py:391
  78.6 22.2 %collective-permute-start.36 = (bf16[96,1024]{1,0:T(8,128)(2,1)S(1)}, bf16[96,1024]{1,0:T(8,128)(2,1)S(1)}, u32[]{:S(2)}, u32[]{:S(2)}) collective-permute-start(bf16[96,1024]{1,0:T(8,128)(2,1)S(1)} %get-tuple-element.50.refs_6_), channel_id=1, source_target_pairs={{0,16},{8,24},{16,0},{24,8},{1,17},{9,25},{17,1},{25,9},{2,18},{10... | collective-permute-start | bytes 589832 | tf_op jit(solution)/shard_map/ppermute | solution.py:391
  80.1 22.6 %collective-permute-start.38 = (bf16[96,1024]{1,0:T(8,128)(2,1)S(1)}, bf16[96,1024]{1,0:T(8,128)(2,1)S(1)}, u32[]{:S(2)}, u32[]{:S(2)}) collective-permute-start(bf16[96,1024]{1,0:T(8,128)(2,1)S(1)} %get-tuple-element.51.refs_7_), channel_id=1, source_target_pairs={{0,24},{8,16},{16,8},{24,0},{1,25},{9,17},{17,9},{25,1},{2,26},{10... | collective-permute-start | bytes 589832 | tf_op jit(solution)/shard_map/ppermute | solution.py:391
  80.1 69.4 %copy-start.2 = (bf16[192,128]{1,0:T(8,128)(2,1)S(1)}, bf16[192,128]{1,0:T(8,128)(2,1)}, u32[]{:S(2)}) copy-start(bf16[192,128]{1,0:T(8,128)(2,1)} %get-tuple-element.35.one_hot_ref) | copy-start | bytes 147460
  97.4 7.5 %collective-permute-start.7 = (bf16[24,4096]{1,0:T(8,128)(2,1)S(1)}, bf16[24,4096]{1,0:T(8,128)(2,1)S(1)}, u32[]{:S(2)}, u32[]{:S(2)}) collective-permute-start(bf16[24,4096]{1,0:T(8,128)(2,1)S(1)} %get-tuple-element.53), channel_id=1, source_target_pairs={{1,0},{0,1},{3,2},{2,3},{5,4},{4,5},{7,6},{6,7},{9,8},{8,9},{11,10... | collective-permute-start | bytes 589832 | tf_op jit(solution)/shard_map/ppermute | solution.py:400
  99.0 7.8 %collective-permute-start.8 = (bf16[24,4096]{1,0:T(8,128)(2,1)S(1)}, bf16[24,4096]{1,0:T(8,128)(2,1)S(1)}, u32[]{:S(2)}, u32[]{:S(2)}) collective-permute-start(bf16[24,4096]{1,0:T(8,128)(2,1)S(1)} %get-tuple-element.54), channel_id=1, source_target_pairs={{2,0},{3,1},{4,2},{5,3},{6,4},{7,5},{0,6},{1,7},{10,8},{11,9},{12,... | collective-permute-start | bytes 589832 | tf_op jit(solution)/shard_map/ppermute | solution.py:400
  100.7 17.9 %collective-permute-start.9 = (bf16[24,4096]{1,0:T(8,128)(2,1)S(1)}, bf16[24,4096]{1,0:T(8,128)(2,1)S(1)}, u32[]{:S(2)}, u32[]{:S(2)}) collective-permute-start(bf16[24,4096]{1,0:T(8,128)(2,1)S(1)} %get-tuple-element.55), channel_id=1, source_target_pairs={{3,0},{2,1},{5,2},{4,3},{7,4},{6,5},{1,6},{0,7},{11,8},{10,9},{13,... | collective-permute-start | bytes 589832 | tf_op jit(solution)/shard_map/ppermute | solution.py:400
  100.7 20.5 %collective-permute-start.10 = (bf16[24,4096]{1,0:T(8,128)(2,1)S(1)}, bf16[24,4096]{1,0:T(8,128)(2,1)S(1)}, u32[]{:S(2)}, u32[]{:S(2)}) collective-permute-start(bf16[24,4096]{1,0:T(8,128)(2,1)S(1)} %get-tuple-element.56), channel_id=1, source_target_pairs={{6,0},{7,1},{0,2},{1,3},{2,4},{3,5},{4,6},{5,7},{14,8},{15,9},{8,1... | collective-permute-start | bytes 589832 | tf_op jit(solution)/shard_map/ppermute | solution.py:400
  102.7 18.6 %collective-permute-start.11 = (bf16[24,4096]{1,0:T(8,128)(2,1)S(1)}, bf16[24,4096]{1,0:T(8,128)(2,1)S(1)}, u32[]{:S(2)}, u32[]{:S(2)}) collective-permute-start(bf16[24,4096]{1,0:T(8,128)(2,1)S(1)} %get-tuple-element.57), channel_id=1, source_target_pairs={{7,0},{6,1},{1,2},{0,3},{3,4},{2,5},{5,6},{4,7},{15,8},{14,9},{9,1... | collective-permute-start | bytes 589832 | tf_op jit(solution)/shard_map/ppermute | solution.py:400
  104.9 31.5 %collective-permute-start.27 = (bf16[72,4096]{1,0:T(8,128)(2,1)S(1)}, bf16[72,4096]{1,0:T(8,128)(2,1)S(1)}, u32[]{:S(2)}, u32[]{:S(2)}) collective-permute-start(bf16[72,4096]{1,0:T(8,128)(2,1)S(1)} %join_rows.4.refs_2_), channel_id=1, source_target_pairs={{0,16},{8,24},{16,0},{24,8},{1,17},{9,25},{17,1},{25,9},{2,18},{10... | collective-permute-start | bytes 1769480 | tf_op jit(solution)/shard_map/ppermute | solution.py:391
  106.8 24.6 %collective-permute-start.12 = (bf16[24,4096]{1,0:T(8,128)(2,1)S(1)}, bf16[24,4096]{1,0:T(8,128)(2,1)S(1)}, u32[]{:S(2)}, u32[]{:S(2)}) collective-permute-start(bf16[24,4096]{1,0:T(8,128)(2,1)S(1)} %get-tuple-element.58), channel_id=1, source_target_pairs={{4,0},{5,1},{6,2},{7,3},{0,4},{1,5},{2,6},{3,7},{12,8},{13,9},{14,... | collective-permute-start | bytes 589832 | tf_op jit(solution)/shard_map/ppermute | solution.py:400
  118.6 13.8 %collective-permute-start.26 = (bf16[24,4096]{1,0:T(8,128)(2,1)S(1)}, bf16[24,4096]{1,0:T(8,128)(2,1)S(1)}, u32[]{:S(2)}, u32[]{:S(2)}) collective-permute-start(bf16[24,4096]{1,0:T(8,128)(2,1)S(1)} %collective-permute-done.15.refs_1_), channel_id=1, source_target_pairs={{0,16},{8,24},{16,0},{24,8},{1,17},{9,25},{17,1},{25,9},{2,18},{10... | collective-permute-start | bytes 589832 | tf_op jit(solution)/shard_map/ppermute | solution.py:391
  121.2 14.2 %collective-permute-start.13 = (bf16[24,4096]{1,0:T(8,128)(2,1)S(1)}, bf16[24,4096]{1,0:T(8,128)(2,1)S(1)}, u32[]{:S(2)}, u32[]{:S(2)}) collective-permute-start(bf16[24,4096]{1,0:T(8,128)(2,1)S(1)} %get-tuple-element.59), channel_id=1, source_target_pairs={{5,0},{4,1},{7,2},{6,3},{1,4},{0,5},{3,6},{2,7},{13,8},{12,9},{15,... | collective-permute-start | bytes 589832 | tf_op jit(solution)/shard_map/ppermute | solution.py:400
  121.2 14.2 %collective-permute-start.22 = (bf16[24,4096]{1,0:T(8,128)(2,1)S(1)}, bf16[24,4096]{1,0:T(8,128)(2,1)S(1)}, u32[]{:S(2)}, u32[]{:S(2)}) collective-permute-start(bf16[24,4096]{1,0:T(8,128)(2,1)S(1)} %collective-permute-done.15.refs_1_), channel_id=1, source_target_pairs={{0,8},{8,0},{16,24},{24,16},{1,9},{9,1},{17,25},{25,17},{2,10},{10... | collective-permute-start | bytes 589832 | tf_op jit(solution)/shard_map/ppermute | solution.py:391
  131.4 12.0 %collective-permute-start.28 = (bf16[48,4096]{1,0:T(8,128)(2,1)S(1)}, bf16[48,4096]{1,0:T(8,128)(2,1)S(1)}, u32[]{:S(2)}, u32[]{:S(2)}) collective-permute-start(bf16[48,4096]{1,0:T(8,128)(2,1)S(1)} %join_rows.5.refs_3_), channel_id=1, source_target_pairs={{0,16},{8,24},{16,0},{24,8},{1,17},{9,25},{17,1},{25,9},{2,18},{10... | collective-permute-start | bytes 1179656 | tf_op jit(solution)/shard_map/ppermute | solution.py:391
  132.4 3.8 %collective-permute-start.30 = (bf16[24,4096]{1,0:T(8,128)(2,1)S(1)}, bf16[24,4096]{1,0:T(8,128)(2,1)S(1)}, u32[]{:S(2)}, u32[]{:S(2)}) collective-permute-start(bf16[24,4096]{1,0:T(8,128)(2,1)S(1)} %collective-permute-done.26.refs_9_), channel_id=1, source_target_pairs={{0,8},{8,0},{16,24},{24,16},{1,9},{9,1},{17,25},{25,17},{2,10},{10... | collective-permute-start | bytes 589832 | tf_op jit(solution)/shard_map/ppermute | solution.py:391
  135.5 7.9 %collective-permute-start.24 = (bf16[48,4096]{1,0:T(8,128)(2,1)S(1)}, bf16[48,4096]{1,0:T(8,128)(2,1)S(1)}, u32[]{:S(2)}, u32[]{:S(2)}) collective-permute-start(bf16[48,4096]{1,0:T(8,128)(2,1)S(1)} %join_rows.5.refs_3_), channel_id=1, source_target_pairs={{0,8},{8,0},{16,24},{24,16},{1,9},{9,1},{17,25},{25,17},{2,10},{10... | collective-permute-start | bytes 1179656 | tf_op jit(solution)/shard_map/ppermute | solution.py:391
  135.5 14.0 %collective-permute-start.25 = (bf16[48,4096]{1,0:T(8,128)(2,1)S(1)}, bf16[48,4096]{1,0:T(8,128)(2,1)S(1)}, u32[]{:S(2)}, u32[]{:S(2)}) collective-permute-start(bf16[48,4096]{1,0:T(8,128)(2,1)S(1)} %join_rows.3.refs_0_), channel_id=1, source_target_pairs={{0,16},{8,24},{16,0},{24,8},{1,17},{9,25},{17,1},{25,9},{2,18},{10... | collective-permute-start | bytes 1179656 | tf_op jit(solution)/shard_map/ppermute | solution.py:391
  136.1 15.1 %collective-permute-start.23 = (bf16[72,4096]{1,0:T(8,128)(2,1)S(1)}, bf16[72,4096]{1,0:T(8,128)(2,1)S(1)}, u32[]{:S(2)}, u32[]{:S(2)}) collective-permute-start(bf16[72,4096]{1,0:T(8,128)(2,1)S(1)} %join_rows.4.refs_2_), channel_id=1, source_target_pairs={{0,8},{8,0},{16,24},{24,16},{1,9},{9,1},{17,25},{25,17},{2,10},{10... | collective-permute-start | bytes 1769480 | tf_op jit(solution)/shard_map/ppermute | solution.py:391
  136.4 14.9 %collective-permute-start.31 = (bf16[72,4096]{1,0:T(8,128)(2,1)S(1)}, bf16[72,4096]{1,0:T(8,128)(2,1)S(1)}, u32[]{:S(2)}, u32[]{:S(2)}) collective-permute-start(bf16[72,4096]{1,0:T(8,128)(2,1)S(1)} %collective-permute-done.27.refs_10_), channel_id=1, source_target_pairs={{0,8},{8,0},{16,24},{24,16},{1,9},{9,1},{17,25},{25,17},{2,10},{10... | collective-permute-start | bytes 1769480 | tf_op jit(solution)/shard_map/ppermute | solution.py:391
  143.4 7.9 %collective-permute-start.21 = (bf16[48,4096]{1,0:T(8,128)(2,1)S(1)}, bf16[48,4096]{1,0:T(8,128)(2,1)S(1)}, u32[]{:S(2)}, u32[]{:S(2)}) collective-permute-start(bf16[48,4096]{1,0:T(8,128)(2,1)S(1)} %join_rows.3.refs_0_), channel_id=1, source_target_pairs={{0,8},{8,0},{16,24},{24,16},{1,9},{9,1},{17,25},{25,17},{2,10},{10... | collective-permute-start | bytes 1179656 | tf_op jit(solution)/shard_map/ppermute | solution.py:391
  143.4 7.9 %collective-permute-start.32 = (bf16[48,4096]{1,0:T(8,128)(2,1)S(1)}, bf16[48,4096]{1,0:T(8,128)(2,1)S(1)}, u32[]{:S(2)}, u32[]{:S(2)}) collective-permute-start(bf16[48,4096]{1,0:T(8,128)(2,1)S(1)} %collective-permute-done.28.refs_11_), channel_id=1, source_target_pairs={{0,8},{8,0},{16,24},{24,16},{1,9},{9,1},{17,25},{25,17},{2,10},{10... | collective-permute-start | bytes 1179656 | tf_op jit(solution)/shard_map/ppermute | solution.py:391
  149.5 1.8 %collective-permute-start.29 = (bf16[48,4096]{1,0:T(8,128)(2,1)S(1)}, bf16[48,4096]{1,0:T(8,128)(2,1)S(1)}, u32[]{:S(2)}, u32[]{:S(2)}) collective-permute-start(bf16[48,4096]{1,0:T(8,128)(2,1)S(1)} %collective-permute-done.25.refs_8_), channel_id=1, source_target_pairs={{0,8},{8,0},{16,24},{24,16},{1,9},{9,1},{17,25},{25,17},{2,10},{10... | collective-permute-start | bytes 1179656 | tf_op jit(solution)/shard_map/ppermute | solution.py:391
where the time goes:
time: 162 us
  waiting for transfers between devices  72.4 us (45%)
  starting transfers between devices  51.3 us (32%)
  Pallas kernels  34.3 us (21%)
  local copies, waits for them, and re-layouts  2.95 us (2%)
    ppermute x21, waiting for transfers between devices, swap_blocks(): got.append(lax.ppermute(blocks[k], 'tower', pairs))  60.1 us
    ppermute x21, starting transfers between devices, swap_blocks(): got.append(lax.ppermute(blocks[k], 'tower', pairs))  40.5 us
    pallas_call x1, Pallas kernels, token_grad(): pl.pallas_call(functools.partial(token_grad_kernel, pieces, len(cot_piece...  17.3 us
    ppermute x18, waiting for transfers between devices, flip_over(): return lax.ppermute(value, axis, [(i, i ^ flip) for i in range(size)])  12.4 us
    ppermute x18, starting transfers between devices, flip_over(): return lax.ppermute(value, axis, [(i, i ^ flip) for i in range(size)])  10.8 us
    pallas_call x1, Pallas kernels, weight_grad_of(): pl.pallas_call(functools.partial(weight_grad_kernel, len(attn_parts), len...  10.5 us
    pallas_call x1, Pallas kernels, dispatch_first(): pl.pallas_call(functools.partial(first_dispatch_kernel, chunks), in_specs...  3.27 us
  transfers between devices with their start and end apart: 39, of which 15 were waited for; matrix products, arithmetic and copies ran while one was open for 0% of the time, Pallas kernels for 13%

commit v1 on v0

--- a/solution.py
+++ b/solution.py
@@ -21,6 +21,10 @@
 
 def grant(mib):
     return pltpu.CompilerParams(vmem_limit_bytes=mib * MIB)
+
+
+def kept_in_hbm(value):
+    return pltpu.with_memory_space_constraint(value, pltpu.HBM)
 
 
 def cost(flops, moved):
@@ -83,8 +87,11 @@
     return jnp.where(slots == place, 1.0, 0.0).astype(BF16)
 
 
-def first_dispatch_kernel(chunks, tower_ref, kinds_hbm, modal_hbm, rows_hbm, one_hot_ref, *refs):
-    out_refs, (kinds_ref, modal_ref, rows_ref, known, arrived) = refs[:NGROUP], refs[NGROUP:]
+def first_dispatch_kernel(
+    chunks, blocks, tower_ref, kinds_hbm, modal_hbm, rows_hbm, one_hot_ref, *refs
+):
+    out_refs, (kinds_ref, modal_ref, rows_ref, known, arrived) = refs[:-5], refs[-5:]
+    first, last = min(blocks) * CAP, (max(blocks) + 1) * CAP
     width = rows_ref.shape[1] // chunks
     tables = [
         pltpu.make_async_copy(kinds_hbm, kinds_ref, known.at[0]),
@@ -105,29 +112,32 @@
     for c in range(chunks):
         columns = pl.ds(c * width, width)
         copies[c].wait()
-        placed = jnp.dot(one_hot_ref[...], rows_ref[:, columns], preferred_element_type=F32)
-        for k, out_ref in enumerate(out_refs):
-            out_ref[:, columns] = placed[k * CAP : (k + 1) * CAP, :].astype(BF16)
-
-
-def dispatch_kernel(one_hot_ref, rows_ref, *out_refs):
+        placed = jnp.dot(
+            one_hot_ref[first:last, :], rows_ref[:, columns], preferred_element_type=F32
+        )
+        for k, out_ref in zip(blocks, out_refs):
+            at = k * CAP - first
+            out_ref[:, columns] = placed[at : at + CAP, :].astype(BF16)
+
+
+def dispatch_kernel(blocks, one_hot_ref, rows_ref, *out_refs):
     placed = jnp.dot(one_hot_ref[...], rows_ref[...], preferred_element_type=F32)
-    for k, out_ref in enumerate(out_refs):
+    for k, out_ref in zip(blocks, out_refs):
         out_ref[...] = placed[k * CAP : (k + 1) * CAP, :].astype(BF16)
 
 
-def dispatch_first(tower_idx, kinds, modal_row, rows):
+def dispatch_first(tower_idx, kinds, modal_row, rows, blocks):
     tokens, width = rows.shape
     chunks = 4
     slots = NGROUP * CAP
     in_smem = pl.BlockSpec(memory_space=pltpu.SMEM)
     in_vmem = pl.BlockSpec(memory_space=pltpu.VMEM)
     out = pl.pallas_call(
-        functools.partial(first_dispatch_kernel, chunks),
+        functools.partial(first_dispatch_kernel, chunks, blocks),
         in_specs=[in_smem] + [pl.BlockSpec(memory_space=pltpu.HBM)] * 3,
-        out_specs=[in_vmem] * (NGROUP + 1),
+        out_specs=[in_vmem] * (len(blocks) + 1),
         out_shape=[jax.ShapeDtypeStruct((slots, tokens), BF16)]
-        + [jax.ShapeDtypeStruct((CAP, width), BF16)] * NGROUP,
+        + [jax.ShapeDtypeStruct((CAP, width), BF16)] * len(blocks),
         scratch_shapes=[
             pltpu.SMEM((NGROUP,), I32),
             pltpu.VMEM((1, tokens), I32),
@@ -136,31 +146,29 @@
             pltpu.SemaphoreType.DMA((chunks,)),
         ],
         cost_estimate=cost(2 * slots * tokens * width, 2 * (tokens + slots) * width),
-        compiler_params=grant(56),
+        compiler_params=grant(12),
         name="dispatch_cot",
-    )(tower_idx, kinds, modal_row, rows)
-    return out[0], list(out[1:])
-
-
-def dispatch_next(one_hot, rows):
+    )(tower_idx, *map(kept_in_hbm, (kinds, modal_row, rows)))
+    return out[0], dict(zip(blocks, out[1:]))
+
+
+def dispatch_next(one_hot, rows, blocks, mib):
     tokens, width = rows.shape
     block = min(1024, width)
     slots = one_hot.shape[0]
-    return list(
-        pl.pallas_call(
-            dispatch_kernel,
-            grid=(width // block,),
-            in_specs=[
-                pl.BlockSpec((slots, tokens), lambda i: (0, 0)),
-                pl.BlockSpec((tokens, block), lambda i: (0, i)),
-            ],
-            out_specs=[pl.BlockSpec((CAP, block), lambda i: (0, i))] * NGROUP,
-            out_shape=[jax.ShapeDtypeStruct((CAP, width), BF16)] * NGROUP,
-            cost_estimate=cost(2 * slots * tokens * width, 2 * (tokens + slots) * width),
-            compiler_params=grant(12),
-            name="dispatch_attn",
-        )(one_hot, rows)
-    )
+    out = pl.pallas_call(
+        functools.partial(dispatch_kernel, blocks),
+        grid=(width // block,),
+        in_specs=[
+            pl.BlockSpec((slots, tokens), lambda i: (0, 0)),
+            pl.BlockSpec((tokens, block), lambda i: (0, i)),
+        ],
+        out_specs=[pl.BlockSpec((CAP, block), lambda i: (0, i))] * len(blocks),
+        out_shape=[jax.ShapeDtypeStruct((CAP, width), BF16)] * len(blocks),
+        cost_estimate=cost(2 * slots * tokens * width, 2 * (tokens + slots) * width),
+        compiler_params=grant(mib),
+    )(one_hot, kept_in_hbm(rows))
+    return dict(zip(blocks, out))
 
 
 def pieces_kernel(count, dp_ref, *refs):
@@ -414,6 +422,7 @@
 COT_PARTS = {"cot_early": (0, 1, 2, 3), "cot_late": (4, 5, 6, 7)}
 ATTN_PARTS = {"attn_a": (0, 1), "attn_b": (2,), "attn_c": (3, 4, 5), "attn_d": (6, 7)}
 LAST = (6, 7)
+FIRST = (2, 3)
 
 
 def small_towers(attn_out, out_cot, modality, group_modality, o_weight):
@@ -421,10 +430,13 @@
     dp_idx = lax.axis_index("dp").astype(I32).reshape(1)
     dp_count = lax.axis_size("dp")
 
+    every = tuple(range(NGROUP))
+    rest = tuple(k for k in every if k not in FIRST)
     one_hot, cot_blocks = dispatch_first(
-        tower_idx.reshape(1), group_modality, modality.reshape(1, -1), out_cot
-    )
-    attn_blocks = dispatch_next(one_hot, attn_out)
+        tower_idx.reshape(1), group_modality, modality.reshape(1, -1), out_cot, FIRST
+    )
+    cot_blocks |= dispatch_next(one_hot, out_cot, rest, 12)
+    attn_blocks = dispatch_next(one_hot, attn_out, every, 56)
     cot_got = swap_blocks(cot_blocks)
     attn_got = swap_blocks(attn_blocks)
     cot_pieces, cot_moved = [], []

time: 162 us -> 161 us (level)
  starting transfers between devices: 51.3 us -> 45.3 us
  Pallas kernels: 34.3 us -> 38.3 us
  waiting for transfers between devices: 72.4 us -> 75.9 us
  local copies, waits for them, and re-layouts: 2.95 us -> 0.01 us
    ppermute x21, starting transfers between devices: 40.5 us -> 34.6 us  [swap_blocks(): got.append(lax.ppermute(blocks[k], 'tower', pairs))]
    pallas_call x2 -> x3, Pallas kernels: 4.51 us -> 8.44 us  [the longest x2 6.56 us: dispatch_next(): pl.pallas_call(functools.partial(dispatch_kernel, blocks), grid=(width //...]
    ppermute x21, waiting for transfers between devices: 60.1 us -> 63.2 us  [swap_blocks(): got.append(lax.ppermute(blocks[k], 'tower', pairs))]
    unnamed x8 -> x6, local copies, waits for them, and re-layouts: 2.95 us -> 0.01 us
  transfers between devices with their start and end apart: 39 -> 39, of which waited for: 15 -> 12; matrix products, arithmetic and copies ran while one was open for 0% -> 0% of each run, Pallas kernels for 13% -> 16%
where the time goes in v1:
time: 161 us; the launch traced here: 160 us
  waiting for transfers between devices  75.9 us (47%)
  starting transfers between devices  45.3 us (28%)
  Pallas kernels  38.3 us (24%)
    ppermute x21, waiting for transfers between devices, swap_blocks(): got.append(lax.ppermute(blocks[k], 'tower', pairs))  63.2 us
    ppermute x21, starting transfers between devices, swap_blocks(): got.append(lax.ppermute(blocks[k], 'tower', pairs))  34.6 us
    pallas_call x1, Pallas kernels, token_grad(): pl.pallas_call(functools.partial(token_grad_kernel, pieces, len(cot_piece...  17.4 us
    ppermute x18, waiting for transfers between devices, flip_over(): return lax.ppermute(value, axis, [(i, i ^ flip) for i in range(size)])  12.6 us
    ppermute x18, starting transfers between devices, flip_over(): return lax.ppermute(value, axis, [(i, i ^ flip) for i in range(size)])  10.7 us
    pallas_call x1, Pallas kernels, weight_grad_of(): pl.pallas_call(functools.partial(weight_grad_kernel, len(attn_parts), len...  10.5 us
    pallas_call x2, Pallas kernels, dispatch_next(): pl.pallas_call(functools.partial(dispatch_kernel, blocks), grid=(width //...  6.56 us
  transfers between devices with their start and end apart: 39, of which 12 were waited for; matrix products, arithmetic and copies ran while one was open for 0% of the time, Pallas kernels for 16%

profile of v1, /device:TPU:0, one launch (start us, length us, event | category | flops | bytes accessed | tf_op | source)
XLA Modules:
  0.0 160.3 jit_solution(8035269738683717833)
XLA Ops:
  0.6 1.9 %dispatch_cot.1 = (bf16[192,128]{1,0:T(8,128)(2,1)S(1)}, bf16[24,4096]{1,0:T(8,128)(2,1)S(1)}, bf16[24,4096]{1,0:T(8,128)(2,1)S(1)}) custom-call(s32[1]{0:T(128)} %bitcast.tower_ref, s32[8]{0:T(128)} %kinds_hbm.1, s32[1,128]{1,0:T(1,128)} %bitcast.3, bf16[128,4096]{1,0:T(8,128)(2,1)} %rows_ref.2), custom_call_target="tpu_custom_call" | custom-call | flops 201326592 | bytes 2621440 | tf_op jit(solution)/shard_map/dispatch_cot/pallas_call | solution.py:135
  2.5 3.1 %collective-permute-start.1 = (bf16[24,4096]{1,0:T(8,128)(2,1)S(1)}, bf16[24,4096]{1,0:T(8,128)(2,1)S(1)}, u32[]{:S(2)}, u32[]{:S(2)}) collective-permute-start(bf16[24,4096]{1,0:T(8,128)(2,1)S(1)} %get-tuple-element.38), channel_id=1, source_target_pairs={{0,2},{1,3},{2,4},{3,5},{4,6},{5,7},{6,0},{7,1},{8,10},{9,11},{10,... | collective-permute-start | bytes 589832 | tf_op jit(solution)/shard_map/ppermute | solution.py:408
  5.6 2.5 %collective-permute-start.2 = (bf16[24,4096]{1,0:T(8,128)(2,1)S(1)}, bf16[24,4096]{1,0:T(8,128)(2,1)S(1)}, u32[]{:S(2)}, u32[]{:S(2)}) collective-permute-start(bf16[24,4096]{1,0:T(8,128)(2,1)S(1)} %get-tuple-element.39), channel_id=1, source_target_pairs={{0,3},{1,2},{2,5},{3,4},{4,7},{5,6},{6,1},{7,0},{8,11},{9,10},{10,... | collective-permute-start | bytes 589832 | tf_op jit(solution)/shard_map/ppermute | solution.py:408
  8.1 2.8 %shard_map.68 = (bf16[24,4096]{1,0:T(8,128)(2,1)S(1)}, bf16[24,4096]{1,0:T(8,128)(2,1)S(1)}, bf16[24,4096]{1,0:T(8,128)(2,1)S(1)}, bf16[24,4096]{1,0:T(8,128)(2,...) custom-call(bf16[192,128]{1,0:T(8,128)(2,1)S(1)} %get-tuple-element.35.one_hot_ref, ...), custom_call_target="tpu_custom_call" | custom-call | flops 201326592 | bytes 2621440 | tf_op jit(solution)/shard_map/pallas_call | solution.py:159
  10.9 0.6 collective-permute-start
  11.5 2.3 %collective-permute-start.3 = (bf16[24,4096]{1,0:T(8,128)(2,1)S(1)}, bf16[24,4096]{1,0:T(8,128)(2,1)S(1)}, u32[]{:S(2)}, u32[]{:S(2)}) collective-permute-start(bf16[24,4096]{1,0:T(8,128)(2,1)S(1)} %get-tuple-element.44), channel_id=1, source_target_pairs={{0,6},{1,7},{2,0},{3,1},{4,2},{5,3},{6,4},{7,5},{8,14},{9,15},{10,... | collective-permute-start | bytes 589832 | tf_op jit(solution)/shard_map/ppermute | solution.py:408
  13.8 1.4 collective-permute-start.4
  15.1 3.8 %shard_map.69 = (bf16[24,4096]{1,0:T(8,128)(2,1)}, bf16[24,4096]{1,0:T(8,128)(2,1)}, bf16[24,4096]{1,0:T(8,128)(2,1)}, bf16[24,4096]{1,0:T(8,128)(2,1)}, bf16[24...) custom-call(bf16[192,128]{1,0:T(8,128)(2,1)} %copy-done, ...), custom_call_target="tpu_custom_call" | custom-call | flops 201326592 | bytes 2621440 | tf_op jit(solution)/shard_map/pallas_call | solution.py:159
  18.9 0.0 collective-permute-done.1.refs_2_
  18.9 0.9 collective-permute-start.5
  19.8 0.0 collective-permute-done.2.refs_3_
  19.8 13.4 %collective-permute-start.6 = (bf16[24,4096]{1,0:T(8,128)(2,1)S(1)}, bf16[24,4096]{1,0:T(8,128)(2,1)S(1)}, u32[]{:S(2)}, u32[]{:S(2)}) collective-permute-start(bf16[24,4096]{1,0:T(8,128)(2,1)S(1)} %get-tuple-element.47), channel_id=1, source_target_pairs={{0,5},{1,4},{2,7},{3,6},{4,1},{5,0},{6,3},{7,2},{8,13},{9,12},{10,... | collective-permute-start | bytes 589832 | tf_op jit(solution)/shard_map/ppermute | solution.py:408
  33.2 0.0 collective-permute-done.refs_1_
  33.2 1.5 collective-permute-start.14
  34.7 0.6 collective-permute-start.16
  35.3 0.1 column_pieces.2
  35.3 11.0 %collective-permute-done.5.refs_2_ = bf16[24,4096]{1,0:T(8,128)(2,1)S(1)} collective-permute-done((bf16[24,4096]{1,0:T(8,128)(2,1)S(1)}, bf16[24,4096]{1,0:T(8,128)(2,1)S(1)}, u32[]{:S(2)}, u32[]{:S(2)}) %collective-permute-start.5) | collective-permute-done | bytes 196640 | tf_op jit(solution)/shard_map/ppermute | solution.py:408
  46.4 0.0 collective-permute-start.17
  46.4 5.3 %collective-permute-done.6.refs_3_ = bf16[24,4096]{1,0:T(8,128)(2,1)S(1)} collective-permute-done((bf16[24,4096]{1,0:T(8,128)(2,1)S(1)}, bf16[24,4096]{1,0:T(8,128)(2,1)S(1)}, u32[]{:S(2)}, u32[]{:S(2)}) %collective-permute-start.6) | collective-permute-done | bytes 196640 | tf_op jit(solution)/shard_map/ppermute | solution.py:408
  51.6 0.0 collective-permute-start.18
  51.7 0.0 collective-permute-done.14.refs_1_
  51.7 0.0 collective-permute-start.19
  51.7 0.0 collective-permute-done.15.refs_1_
  51.7 2.7 %collective-permute-start.20 = (bf16[24,4096]{1,0:T(8,128)(2,1)}, bf16[24,4096]{1,0:T(8,128)(2,1)S(1)}, u32[]{:S(2)}, u32[]{:S(2)}) collective-permute-start(bf16[24,4096]{1,0:T(8,128)(2,1)} %get-tuple-element.67), channel_id=1, source_target_pairs={{0,5},{1,4},{2,7},{3,6},{4,1},{5,0},{6,3},{7,2},{8,13},{9,12},{10,... | collective-permute-start | bytes 589832 | tf_op jit(solution)/shard_map/ppermute | solution.py:408
  54.4 0.1 column_pieces.3
  54.5 0.3 collective-permute-done.17.refs_1_
  54.8 1.5 collective-permute-start.35
  56.3 3.5 %collective-permute-done.18.refs_2_ = bf16[24,4096]{1,0:T(8,128)(2,1)S(1)} collective-permute-done((bf16[24,4096]{1,0:T(8,128)(2,1)}, bf16[24,4096]{1,0:T(8,128)(2,1)S(1)}, u32[]{:S(2)}, u32[]{:S(2)}) %collective-permute-start.18) | collective-permute-done | bytes 196640 | tf_op jit(solution)/shard_map/ppermute | solution.py:408
  59.9 0.6 collective-permute-start.37
  60.5 11.2 %collective-permute-done.19.refs_0_ = bf16[24,4096]{1,0:T(8,128)(2,1)S(1)} collective-permute-done((bf16[24,4096]{1,0:T(8,128)(2,1)}, bf16[24,4096]{1,0:T(8,128)(2,1)S(1)}, u32[]{:S(2)}, u32[]{:S(2)}) %collective-permute-start.19) | collective-permute-done | bytes 196640 | tf_op jit(solution)/shard_map/ppermute | solution.py:408
  71.7 5.1 %collective-permute-done.20.refs_1_ = bf16[24,4096]{1,0:T(8,128)(2,1)S(1)} collective-permute-done((bf16[24,4096]{1,0:T(8,128)(2,1)}, bf16[24,4096]{1,0:T(8,128)(2,1)S(1)}, u32[]{:S(2)}, u32[]{:S(2)}) %collective-permute-start.20) | collective-permute-done | bytes 196640 | tf_op jit(solution)/shard_map/ppermute | solution.py:408
  76.7 1.5 collective-permute-start.36
  78.3 0.0 collective-permute-start.38
  78.3 17.4 %token_grad.1 = (bf16[24,4096]{1,0:T(8,128)(2,1)S(1)}, bf16[24,4096]{1,0:T(8,128)(2,1)S(1)}, bf16[24,4096]{1,0:T(8,128)(2,1)S(1)}, bf16[24,4096]{1,0:T(8,128)(2,...) custom-call(s32[1]{0:T(128)} %bitcast.2.dp_ref, ...), custom_call_target="tpu_custom_call" | custom-call | flops 6442450944 | bytes 36700160 | tf_op jit(solution)/shard_map/token_grad/pallas_call | solution.py:233
  95.7 0.0 collective-permute-done.35.refs_20_
  95.7 0.6 collective-permute-start.7
  96.3 1.7 %collective-permute-start.8 = (bf16[24,4096]{1,0:T(8,128)(2,1)S(1)}, bf16[24,4096]{1,0:T(8,128)(2,1)S(1)}, u32[]{:S(2)}, u32[]{:S(2)}) collective-permute-start(bf16[24,4096]{1,0:T(8,128)(2,1)S(1)} %get-tuple-element.54), channel_id=1, source_target_pairs={{2,0},{3,1},{4,2},{5,3},{6,4},{7,5},{0,6},{1,7},{10,8},{11,9},{12,... | collective-permute-start | bytes 589832 | tf_op jit(solution)/shard_map/ppermute | solution.py:408
  97.9 1.0 collective-permute-start.9
  98.9 0.0 collective-permute-done.36.refs_21_
  98.9 2.0 %collective-permute-start.10 = (bf16[24,4096]{1,0:T(8,128)(2,1)S(1)}, bf16[24,4096]{1,0:T(8,128)(2,1)S(1)}, u32[]{:S(2)}, u32[]{:S(2)}) collective-permute-start(bf16[24,4096]{1,0:T(8,128)(2,1)S(1)} %get-tuple-element.56), channel_id=1, source_target_pairs={{6,0},{7,1},{0,2},{1,3},{2,4},{3,5},{4,6},{5,7},{14,8},{15,9},{8,1... | collective-permute-start | bytes 589832 | tf_op jit(solution)/shard_map/ppermute | solution.py:408
  100.9 0.0 collective-permute-done.38.refs_23_
  100.9 0.3 collective-permute-start.11
  101.3 1.8 %collective-permute-done.7.refs_1_ = bf16[24,4096]{1,0:T(8,128)(2,1)S(1)} collective-permute-done((bf16[24,4096]{1,0:T(8,128)(2,1)S(1)}, bf16[24,4096]{1,0:T(8,128)(2,1)S(1)}, u32[]{:S(2)}, u32[]{:S(2)}) %collective-permute-start.7) | collective-permute-done | bytes 196640 | tf_op jit(solution)/shard_map/ppermute | solution.py:408
  103.1 1.5 collective-permute-start.27
  104.6 0.0 collective-permute-done.8.refs_2_
  104.6 0.2 collective-permute-start.12
  104.8 12.8 %collective-permute-done.9.refs_3_ = bf16[24,4096]{1,0:T(8,128)(2,1)S(1)} collective-permute-done((bf16[24,4096]{1,0:T(8,128)(2,1)S(1)}, bf16[24,4096]{1,0:T(8,128)(2,1)S(1)}, u32[]{:S(2)}, u32[]{:S(2)}) %collective-permute-start.9) | collective-permute-done | bytes 196640 | tf_op jit(solution)/shard_map/ppermute | solution.py:408
  117.6 1.7 %collective-permute-start.26 = (bf16[24,4096]{1,0:T(8,128)(2,1)S(1)}, bf16[24,4096]{1,0:T(8,128)(2,1)S(1)}, u32[]{:S(2)}, u32[]{:S(2)}) collective-permute-start(bf16[24,4096]{1,0:T(8,128)(2,1)S(1)} %collective-permute-done.15.refs_1_), channel_id=1, source_target_pairs={{0,16},{8,24},{16,0},{24,8},{1,17},{9,25},{17,1},{25,9},{2,18},{10... | collective-permute-start | bytes 589832 | tf_op jit(solution)/shard_map/ppermute | solution.py:399
  119.4 0.1 collective-permute-start.22
  119.5 9.2 %collective-permute-done.12.refs_0_ = bf16[24,4096]{1,0:T(8,128)(2,1)S(1)} collective-permute-done((bf16[24,4096]{1,0:T(8,128)(2,1)S(1)}, bf16[24,4096]{1,0:T(8,128)(2,1)S(1)}, u32[]{:S(2)}, u32[]{:S(2)}) %collective-permute-start.12) | collective-permute-done | bytes 196640 | tf_op jit(solution)/shard_map/ppermute | solution.py:408
  128.7 1.5 collective-permute-start.28
  130.1 0.0 collective-permute-done.26.refs_9_
  130.1 0.0 collective-permute-start.30
  130.1 3.0 %collective-permute-done.13.refs_1_ = bf16[24,4096]{1,0:T(8,128)(2,1)S(1)} collective-permute-done((bf16[24,4096]{1,0:T(8,128)(2,1)S(1)}, bf16[24,4096]{1,0:T(8,128)(2,1)S(1)}, u32[]{:S(2)}, u32[]{:S(2)}) %collective-permute-start.13) | collective-permute-done | bytes 196640 | tf_op jit(solution)/shard_map/ppermute | solution.py:408
  133.2 0.0 collective-permute-start.24
  133.2 1.2 collective-permute-start.25
  134.4 0.2 collective-permute-start.23
  134.6 0.3 collective-permute-start.31
  134.9 5.8 %collective-permute-done.28.refs_11_ = bf16[48,4096]{1,0:T(8,128)(2,1)S(1)} collective-permute-done((bf16[48,4096]{1,0:T(8,128)(2,1)S(1)}, bf16[48,4096]{1,0:T(8,128)(2,1)S(1)}, u32[]{:S(2)}, u32[]{:S(2)}) %collective-permute-start.28) | collective-permute-done | bytes 393248 | tf_op jit(solution)/shard_map/ppermute | solution.py:399
  140.7 0.5 collective-permute-start.32
  141.2 6.8 %collective-permute-done.25.refs_8_ = bf16[48,4096]{1,0:T(8,128)(2,1)S(1)} collective-permute-done((bf16[48,4096]{1,0:T(8,128)(2,1)S(1)}, bf16[48,4096]{1,0:T(8,128)(2,1)S(1)}, u32[]{:S(2)}, u32[]{:S(2)}) %collective-permute-start.25) | collective-permute-done | bytes 393248 | tf_op jit(solution)/shard_map/ppermute | solution.py:399
  148.0 0.5 combine_first.1.partial_ref
  148.5 1.3 combine_last.1
  149.8 10.5 %weight_grad.1 = bf16[4096,1024]{1,0:T(8,128)(2,1)} custom-call(bf16[48,4096]{1,0:T(8,128)(2,1)S(1)} %join_rows.3.refs_0_, bf16[24,4096]{1,0:T(8,128)(2,1)S(1)} %collective-permute-done.15.refs_1_, bf16[72,4096]{1,0:T(8,128)(2,1)S(1)} %join_rows.4.refs_2_, bf16[48,4096]{1,0:T(8,128)(2,1)S(1)} %join_rows.5.refs_3_, ...), custom_call_target="tpu_custom_call" | custom-call | flops 6442450944 | bytes 16252928 | tf_op jit(solution)/shard_map/weight_grad/pallas_call | solution.py:381
  (32 shorter events, 0.2 us)
Async XLA Ops:
  2.5 12.6 %copy-start = (bf16[192,128]{1,0:T(8,128)(2,1)}, bf16[192,128]{1,0:T(8,128)(2,1)S(1)}, u32[]{:S(2)}) copy-start(bf16[192,128]{1,0:T(8,128)(2,1)S(1)} %get-tuple-element.35.one_hot_ref) | copy-start | bytes 147460
  2.5 16.4 %collective-permute-start.1 = (bf16[24,4096]{1,0:T(8,128)(2,1)S(1)}, bf16[24,4096]{1,0:T(8,128)(2,1)S(1)}, u32[]{:S(2)}, u32[]{:S(2)}) collective-permute-start(bf16[24,4096]{1,0:T(8,128)(2,1)S(1)} %get-tuple-element.38), channel_id=1, source_target_pairs={{0,2},{1,3},{2,4},{3,5},{4,6},{5,7},{6,0},{7,1},{8,10},{9,11},{10,... | collective-permute-start | bytes 589832 | tf_op jit(solution)/shard_map/ppermute | solution.py:408
  5.6 14.2 %collective-permute-start.2 = (bf16[24,4096]{1,0:T(8,128)(2,1)S(1)}, bf16[24,4096]{1,0:T(8,128)(2,1)S(1)}, u32[]{:S(2)}, u32[]{:S(2)}) collective-permute-start(bf16[24,4096]{1,0:T(8,128)(2,1)S(1)} %get-tuple-element.39), channel_id=1, source_target_pairs={{0,3},{1,2},{2,5},{3,4},{4,7},{5,6},{6,1},{7,0},{8,11},{9,10},{10,... | collective-permute-start | bytes 589832 | tf_op jit(solution)/shard_map/ppermute | solution.py:408
  10.9 22.3 %collective-permute-start = (bf16[24,4096]{1,0:T(8,128)(2,1)S(1)}, bf16[24,4096]{1,0:T(8,128)(2,1)S(1)}, u32[]{:S(2)}, u32[]{:S(2)}) collective-permute-start(bf16[24,4096]{1,0:T(8,128)(2,1)S(1)} %get-tuple-element.37), channel_id=1, source_target_pairs={{0,1},{1,0},{2,3},{3,2},{4,5},{5,4},{6,7},{7,6},{8,9},{9,8},{10,11... | collective-permute-start | bytes 589832 | tf_op jit(solution)/shard_map/ppermute | solution.py:408
  11.5 23.2 %collective-permute-start.3 = (bf16[24,4096]{1,0:T(8,128)(2,1)S(1)}, bf16[24,4096]{1,0:T(8,128)(2,1)S(1)}, u32[]{:S(2)}, u32[]{:S(2)}) collective-permute-start(bf16[24,4096]{1,0:T(8,128)(2,1)S(1)} %get-tuple-element.44), channel_id=1, source_target_pairs={{0,6},{1,7},{2,0},{3,1},{4,2},{5,3},{6,4},{7,5},{8,14},{9,15},{10,... | collective-permute-start | bytes 589832 | tf_op jit(solution)/shard_map/ppermute | solution.py:408
  13.8 20.9 %collective-permute-start.4 = (bf16[24,4096]{1,0:T(8,128)(2,1)S(1)}, bf16[24,4096]{1,0:T(8,128)(2,1)S(1)}, u32[]{:S(2)}, u32[]{:S(2)}) collective-permute-start(bf16[24,4096]{1,0:T(8,128)(2,1)S(1)} %get-tuple-element.45), channel_id=1, source_target_pairs={{0,7},{1,6},{2,1},{3,0},{4,3},{5,2},{6,5},{7,4},{8,15},{9,14},{10,... | collective-permute-start | bytes 589832 | tf_op jit(solution)/shard_map/ppermute | solution.py:408
  18.9 27.4 %collective-permute-start.5 = (bf16[24,4096]{1,0:T(8,128)(2,1)S(1)}, bf16[24,4096]{1,0:T(8,128)(2,1)S(1)}, u32[]{:S(2)}, u32[]{:S(2)}) collective-permute-start(bf16[24,4096]{1,0:T(8,128)(2,1)S(1)} %get-tuple-element.46), channel_id=1, source_target_pairs={{0,4},{1,5},{2,6},{3,7},{4,0},{5,1},{6,2},{7,3},{8,12},{9,13},{10,... | collective-permute-start | bytes 589832 | tf_op jit(solution)/shard_map/ppermute | solution.py:408
  19.8 31.8 %collective-permute-start.6 = (bf16[24,4096]{1,0:T(8,128)(2,1)S(1)}, bf16[24,4096]{1,0:T(8,128)(2,1)S(1)}, u32[]{:S(2)}, u32[]{:S(2)}) collective-permute-start(bf16[24,4096]{1,0:T(8,128)(2,1)S(1)} %get-tuple-element.47), channel_id=1, source_target_pairs={{0,5},{1,4},{2,7},{3,6},{4,1},{5,0},{6,3},{7,2},{8,13},{9,12},{10,... | collective-permute-start | bytes 589832 | tf_op jit(solution)/shard_map/ppermute | solution.py:408
  33.2 18.4 %collective-permute-start.14 = (bf16[24,4096]{1,0:T(8,128)(2,1)}, bf16[24,4096]{1,0:T(8,128)(2,1)S(1)}, u32[]{:S(2)}, u32[]{:S(2)}) collective-permute-start(bf16[24,4096]{1,0:T(8,128)(2,1)} %get-tuple-element.61), channel_id=1, source_target_pairs={{0,1},{1,0},{2,3},{3,2},{4,5},{5,4},{6,7},{7,6},{8,9},{9,8},{10,11... | collective-permute-start | bytes 589832 | tf_op jit(solution)/shard_map/ppermute | solution.py:408
  34.7 17.0 %collective-permute-start.15 = (bf16[24,4096]{1,0:T(8,128)(2,1)}, bf16[24,4096]{1,0:T(8,128)(2,1)S(1)}, u32[]{:S(2)}, u32[]{:S(2)}) collective-permute-start(bf16[24,4096]{1,0:T(8,128)(2,1)} %get-tuple-element.62), channel_id=1, source_target_pairs={{0,2},{1,3},{2,4},{3,5},{4,6},{5,7},{6,0},{7,1},{8,10},{9,11},{10,... | collective-permute-start | bytes 589832 | tf_op jit(solution)/shard_map/ppermute | solution.py:408
  34.7 19.7 %collective-permute-start.16 = (bf16[24,4096]{1,0:T(8,128)(2,1)}, bf16[24,4096]{1,0:T(8,128)(2,1)S(1)}, u32[]{:S(2)}, u32[]{:S(2)}) collective-permute-start(bf16[24,4096]{1,0:T(8,128)(2,1)} %get-tuple-element.63), channel_id=1, source_target_pairs={{0,3},{1,2},{2,5},{3,4},{4,7},{5,6},{6,1},{7,0},{8,11},{9,10},{10,... | collective-permute-start | bytes 589832 | tf_op jit(solution)/shard_map/ppermute | solution.py:408
  46.4 8.4 %collective-permute-start.17 = (bf16[24,4096]{1,0:T(8,128)(2,1)}, bf16[24,4096]{1,0:T(8,128)(2,1)S(1)}, u32[]{:S(2)}, u32[]{:S(2)}) collective-permute-start(bf16[24,4096]{1,0:T(8,128)(2,1)} %get-tuple-element.64), channel_id=1, source_target_pairs={{0,6},{1,7},{2,0},{3,1},{4,2},{5,3},{6,4},{7,5},{8,14},{9,15},{10,... | collective-permute-start | bytes 589832 | tf_op jit(solution)/shard_map/ppermute | solution.py:408
  51.6 8.2 %collective-permute-start.18 = (bf16[24,4096]{1,0:T(8,128)(2,1)}, bf16[24,4096]{1,0:T(8,128)(2,1)S(1)}, u32[]{:S(2)}, u32[]{:S(2)}) collective-permute-start(bf16[24,4096]{1,0:T(8,128)(2,1)} %get-tuple-element.65), channel_id=1, source_target_pairs={{0,7},{1,6},{2,1},{3,0},{4,3},{5,2},{6,5},{7,4},{8,15},{9,14},{10,... | collective-permute-start | bytes 589832 | tf_op jit(solution)/shard_map/ppermute | solution.py:408
  51.7 20.0 %collective-permute-start.19 = (bf16[24,4096]{1,0:T(8,128)(2,1)}, bf16[24,4096]{1,0:T(8,128)(2,1)S(1)}, u32[]{:S(2)}, u32[]{:S(2)}) collective-permute-start(bf16[24,4096]{1,0:T(8,128)(2,1)} %get-tuple-element.66), channel_id=1, source_target_pairs={{0,4},{1,5},{2,6},{3,7},{4,0},{5,1},{6,2},{7,3},{8,12},{9,13},{10,... | collective-permute-start | bytes 589832 | tf_op jit(solution)/shard_map/ppermute | solution.py:408
  51.7 25.1 %collective-permute-start.20 = (bf16[24,4096]{1,0:T(8,128)(2,1)}, bf16[24,4096]{1,0:T(8,128)(2,1)S(1)}, u32[]{:S(2)}, u32[]{:S(2)}) collective-permute-start(bf16[24,4096]{1,0:T(8,128)(2,1)} %get-tuple-element.67), channel_id=1, source_target_pairs={{0,5},{1,4},{2,7},{3,6},{4,1},{5,0},{6,3},{7,2},{8,13},{9,12},{10,... | collective-permute-start | bytes 589832 | tf_op jit(solution)/shard_map/ppermute | solution.py:408
  54.4 23.8 %collective-permute-start.33 = (bf16[96,1024]{1,0:T(8,128)(2,1)S(1)}, bf16[96,1024]{1,0:T(8,128)(2,1)S(1)}, u32[]{:S(2)}, u32[]{:S(2)}) collective-permute-start(bf16[96,1024]{1,0:T(8,128)(2,1)S(1)} %get-tuple-element.41.refs_1_), channel_id=1, source_target_pairs={{0,8},{8,0},{16,24},{24,16},{1,9},{9,1},{17,25},{25,17},{2,10},{10... | collective-permute-start | bytes 589832 | tf_op jit(solution)/shard_map/ppermute | solution.py:399
  54.8 40.9 %collective-permute-start.35 = (bf16[96,1024]{1,0:T(8,128)(2,1)S(1)}, bf16[96,1024]{1,0:T(8,128)(2,1)S(1)}, u32[]{:S(2)}, u32[]{:S(2)}) collective-permute-start(bf16[96,1024]{1,0:T(8,128)(2,1)S(1)} %get-tuple-element.42.refs_2_), channel_id=1, source_target_pairs={{0,16},{8,24},{16,0},{24,8},{1,17},{9,25},{17,1},{25,9},{2,18},{10... | collective-permute-start | bytes 589832 | tf_op jit(solution)/shard_map/ppermute | solution.py:399
  59.9 36.4 %collective-permute-start.37 = (bf16[96,1024]{1,0:T(8,128)(2,1)S(1)}, bf16[96,1024]{1,0:T(8,128)(2,1)S(1)}, u32[]{:S(2)}, u32[]{:S(2)}) collective-permute-start(bf16[96,1024]{1,0:T(8,128)(2,1)S(1)} %get-tuple-element.43.refs_3_), channel_id=1, source_target_pairs={{0,24},{8,16},{16,8},{24,0},{1,25},{9,17},{17,9},{25,1},{2,26},{10... | collective-permute-start | bytes 589832 | tf_op jit(solution)/shard_map/ppermute | solution.py:399
  71.7 26.3 %collective-permute-start.34 = (bf16[96,1024]{1,0:T(8,128)(2,1)S(1)}, bf16[96,1024]{1,0:T(8,128)(2,1)S(1)}, u32[]{:S(2)}, u32[]{:S(2)}) collective-permute-start(bf16[96,1024]{1,0:T(8,128)(2,1)S(1)} %get-tuple-element.49.refs_5_), channel_id=1, source_target_pairs={{0,8},{8,0},{16,24},{24,16},{1,9},{9,1},{17,25},{25,17},{2,10},{10... | collective-permute-start | bytes 589832 | tf_op jit(solution)/shard_map/ppermute | solution.py:399
  76.7 22.2 %collective-permute-start.36 = (bf16[96,1024]{1,0:T(8,128)(2,1)S(1)}, bf16[96,1024]{1,0:T(8,128)(2,1)S(1)}, u32[]{:S(2)}, u32[]{:S(2)}) collective-permute-start(bf16[96,1024]{1,0:T(8,128)(2,1)S(1)} %get-tuple-element.50.refs_6_), channel_id=1, source_target_pairs={{0,16},{8,24},{16,0},{24,8},{1,17},{9,25},{17,1},{25,9},{2,18},{10... | collective-permute-start | bytes 589832 | tf_op jit(solution)/shard_map/ppermute | solution.py:399
  78.3 22.6 %collective-permute-start.38 = (bf16[96,1024]{1,0:T(8,128)(2,1)S(1)}, bf16[96,1024]{1,0:T(8,128)(2,1)S(1)}, u32[]{:S(2)}, u32[]{:S(2)}) collective-permute-start(bf16[96,1024]{1,0:T(8,128)(2,1)S(1)} %get-tuple-element.51.refs_7_), channel_id=1, source_target_pairs={{0,24},{8,16},{16,8},{24,0},{1,25},{9,17},{17,9},{25,1},{2,26},{10... | collective-permute-start | bytes 589832 | tf_op jit(solution)/shard_map/ppermute | solution.py:399
  78.3 41.2 %copy-start.2 = (bf16[24,4096]{1,0:T(8,128)(2,1)S(1)}, bf16[24,4096]{1,0:T(8,128)(2,1)}, u32[]{:S(2)}) copy-start(bf16[24,4096]{1,0:T(8,128)(2,1)} %get-tuple-element.60.refs_0_) | copy-start | bytes 589828
  78.3 69.7 %copy-start.1 = (bf16[192,128]{1,0:T(8,128)(2,1)S(1)}, bf16[192,128]{1,0:T(8,128)(2,1)}, u32[]{:S(2)}) copy-start(bf16[192,128]{1,0:T(8,128)(2,1)} %copy-done) | copy-start | bytes 147460
  95.7 7.4 %collective-permute-start.7 = (bf16[24,4096]{1,0:T(8,128)(2,1)S(1)}, bf16[24,4096]{1,0:T(8,128)(2,1)S(1)}, u32[]{:S(2)}, u32[]{:S(2)}) collective-permute-start(bf16[24,4096]{1,0:T(8,128)(2,1)S(1)} %get-tuple-element.53), channel_id=1, source_target_pairs={{1,0},{0,1},{3,2},{2,3},{5,4},{4,5},{7,6},{6,7},{9,8},{8,9},{11,10... | collective-permute-start | bytes 589832 | tf_op jit(solution)/shard_map/ppermute | solution.py:408
  96.3 8.4 %collective-permute-start.8 = (bf16[24,4096]{1,0:T(8,128)(2,1)S(1)}, bf16[24,4096]{1,0:T(8,128)(2,1)S(1)}, u32[]{:S(2)}, u32[]{:S(2)}) collective-permute-start(bf16[24,4096]{1,0:T(8,128)(2,1)S(1)} %get-tuple-element.54), channel_id=1, source_target_pairs={{2,0},{3,1},{4,2},{5,3},{6,4},{7,5},{0,6},{1,7},{10,8},{11,9},{12,... | collective-permute-start | bytes 589832 | tf_op jit(solution)/shard_map/ppermute | solution.py:408
  97.9 19.7 %collective-permute-start.9 = (bf16[24,4096]{1,0:T(8,128)(2,1)S(1)}, bf16[24,4096]{1,0:T(8,128)(2,1)S(1)}, u32[]{:S(2)}, u32[]{:S(2)}) collective-permute-start(bf16[24,4096]{1,0:T(8,128)(2,1)S(1)} %get-tuple-element.55), channel_id=1, source_target_pairs={{3,0},{2,1},{5,2},{4,3},{7,4},{6,5},{1,6},{0,7},{11,8},{10,9},{13,... | collective-permute-start | bytes 589832 | tf_op jit(solution)/shard_map/ppermute | solution.py:408
  98.9 20.4 %collective-permute-start.10 = (bf16[24,4096]{1,0:T(8,128)(2,1)S(1)}, bf16[24,4096]{1,0:T(8,128)(2,1)S(1)}, u32[]{:S(2)}, u32[]{:S(2)}) collective-permute-start(bf16[24,4096]{1,0:T(8,128)(2,1)S(1)} %get-tuple-element.56), channel_id=1, source_target_pairs={{6,0},{7,1},{0,2},{1,3},{2,4},{3,5},{4,6},{5,7},{14,8},{15,9},{8,1... | collective-permute-start | bytes 589832 | tf_op jit(solution)/shard_map/ppermute | solution.py:408
  100.9 18.4 %collective-permute-start.11 = (bf16[24,4096]{1,0:T(8,128)(2,1)S(1)}, bf16[24,4096]{1,0:T(8,128)(2,1)S(1)}, u32[]{:S(2)}, u32[]{:S(2)}) collective-permute-start(bf16[24,4096]{1,0:T(8,128)(2,1)S(1)} %get-tuple-element.57), channel_id=1, source_target_pairs={{7,0},{6,1},{1,2},{0,3},{3,4},{2,5},{5,6},{4,7},{15,8},{14,9},{9,1... | collective-permute-start | bytes 589832 | tf_op jit(solution)/shard_map/ppermute | solution.py:408
  103.1 31.5 %collective-permute-start.27 = (bf16[72,4096]{1,0:T(8,128)(2,1)S(1)}, bf16[72,4096]{1,0:T(8,128)(2,1)S(1)}, u32[]{:S(2)}, u32[]{:S(2)}) collective-permute-start(bf16[72,4096]{1,0:T(8,128)(2,1)S(1)} %join_rows.4.refs_2_), channel_id=1, source_target_pairs={{0,16},{8,24},{16,0},{24,8},{1,17},{9,25},{17,1},{25,9},{2,18},{10... | collective-permute-start | bytes 1769480 | tf_op jit(solution)/shard_map/ppermute | solution.py:399
  104.6 24.0 %collective-permute-start.12 = (bf16[24,4096]{1,0:T(8,128)(2,1)S(1)}, bf16[24,4096]{1,0:T(8,128)(2,1)S(1)}, u32[]{:S(2)}, u32[]{:S(2)}) collective-permute-start(bf16[24,4096]{1,0:T(8,128)(2,1)S(1)} %get-tuple-element.58), channel_id=1, source_target_pairs={{4,0},{5,1},{6,2},{7,3},{0,4},{1,5},{2,6},{3,7},{12,8},{13,9},{14,... | collective-permute-start | bytes 589832 | tf_op jit(solution)/shard_map/ppermute | solution.py:408
  117.6 12.5 %collective-permute-start.26 = (bf16[24,4096]{1,0:T(8,128)(2,1)S(1)}, bf16[24,4096]{1,0:T(8,128)(2,1)S(1)}, u32[]{:S(2)}, u32[]{:S(2)}) collective-permute-start(bf16[24,4096]{1,0:T(8,128)(2,1)S(1)} %collective-permute-done.15.refs_1_), channel_id=1, source_target_pairs={{0,16},{8,24},{16,0},{24,8},{1,17},{9,25},{17,1},{25,9},{2,18},{10... | collective-permute-start | bytes 589832 | tf_op jit(solution)/shard_map/ppermute | solution.py:399
  119.3 13.8 %collective-permute-start.13 = (bf16[24,4096]{1,0:T(8,128)(2,1)S(1)}, bf16[24,4096]{1,0:T(8,128)(2,1)S(1)}, u32[]{:S(2)}, u32[]{:S(2)}) collective-permute-start(bf16[24,4096]{1,0:T(8,128)(2,1)S(1)} %get-tuple-element.59), channel_id=1, source_target_pairs={{5,0},{4,1},{7,2},{6,3},{1,4},{0,5},{3,6},{2,7},{13,8},{12,9},{15,... | collective-permute-start | bytes 589832 | tf_op jit(solution)/shard_map/ppermute | solution.py:408
  119.4 13.8 %collective-permute-start.22 = (bf16[24,4096]{1,0:T(8,128)(2,1)S(1)}, bf16[24,4096]{1,0:T(8,128)(2,1)S(1)}, u32[]{:S(2)}, u32[]{:S(2)}) collective-permute-start(bf16[24,4096]{1,0:T(8,128)(2,1)S(1)} %collective-permute-done.15.refs_1_), channel_id=1, source_target_pairs={{0,8},{8,0},{16,24},{24,16},{1,9},{9,1},{17,25},{25,17},{2,10},{10... | collective-permute-start | bytes 589832 | tf_op jit(solution)/shard_map/ppermute | solution.py:399
  128.7 12.0 %collective-permute-start.28 = (bf16[48,4096]{1,0:T(8,128)(2,1)S(1)}, bf16[48,4096]{1,0:T(8,128)(2,1)S(1)}, u32[]{:S(2)}, u32[]{:S(2)}) collective-permute-start(bf16[48,4096]{1,0:T(8,128)(2,1)S(1)} %join_rows.5.refs_3_), channel_id=1, source_target_pairs={{0,16},{8,24},{16,0},{24,8},{1,17},{9,25},{17,1},{25,9},{2,18},{10... | collective-permute-start | bytes 1179656 | tf_op jit(solution)/shard_map/ppermute | solution.py:399
  130.1 4.3 %collective-permute-start.30 = (bf16[24,4096]{1,0:T(8,128)(2,1)S(1)}, bf16[24,4096]{1,0:T(8,128)(2,1)S(1)}, u32[]{:S(2)}, u32[]{:S(2)}) collective-permute-start(bf16[24,4096]{1,0:T(8,128)(2,1)S(1)} %collective-permute-done.26.refs_9_), channel_id=1, source_target_pairs={{0,8},{8,0},{16,24},{24,16},{1,9},{9,1},{17,25},{25,17},{2,10},{10... | collective-permute-start | bytes 589832 | tf_op jit(solution)/shard_map/ppermute | solution.py:399
  133.2 7.5 %collective-permute-start.24 = (bf16[48,4096]{1,0:T(8,128)(2,1)S(1)}, bf16[48,4096]{1,0:T(8,128)(2,1)S(1)}, u32[]{:S(2)}, u32[]{:S(2)}) collective-permute-start(bf16[48,4096]{1,0:T(8,128)(2,1)S(1)} %join_rows.5.refs_3_), channel_id=1, source_target_pairs={{0,8},{8,0},{16,24},{24,16},{1,9},{9,1},{17,25},{25,17},{2,10},{10... | collective-permute-start | bytes 1179656 | tf_op jit(solution)/shard_map/ppermute | solution.py:399
  133.2 14.8 %collective-permute-start.25 = (bf16[48,4096]{1,0:T(8,128)(2,1)S(1)}, bf16[48,4096]{1,0:T(8,128)(2,1)S(1)}, u32[]{:S(2)}, u32[]{:S(2)}) collective-permute-start(bf16[48,4096]{1,0:T(8,128)(2,1)S(1)} %join_rows.3.refs_0_), channel_id=1, source_target_pairs={{0,16},{8,24},{16,0},{24,8},{1,17},{9,25},{17,1},{25,9},{2,18},{10... | collective-permute-start | bytes 1179656 | tf_op jit(solution)/shard_map/ppermute | solution.py:399
  134.4 15.4 %collective-permute-start.23 = (bf16[72,4096]{1,0:T(8,128)(2,1)S(1)}, bf16[72,4096]{1,0:T(8,128)(2,1)S(1)}, u32[]{:S(2)}, u32[]{:S(2)}) collective-permute-start(bf16[72,4096]{1,0:T(8,128)(2,1)S(1)} %join_rows.4.refs_2_), channel_id=1, source_target_pairs={{0,8},{8,0},{16,24},{24,16},{1,9},{9,1},{17,25},{25,17},{2,10},{10... | collective-permute-start | bytes 1769480 | tf_op jit(solution)/shard_map/ppermute | solution.py:399
  134.6 15.2 %collective-permute-start.31 = (bf16[72,4096]{1,0:T(8,128)(2,1)S(1)}, bf16[72,4096]{1,0:T(8,128)(2,1)S(1)}, u32[]{:S(2)}, u32[]{:S(2)}) collective-permute-start(bf16[72,4096]{1,0:T(8,128)(2,1)S(1)} %collective-permute-done.27.refs_10_), channel_id=1, source_target_pairs={{0,8},{8,0},{16,24},{24,16},{1,9},{9,1},{17,25},{25,17},{2,10},{10... | collective-permute-start | bytes 1769480 | tf_op jit(solution)/shard_map/ppermute | solution.py:399
  140.7 9.1 %collective-permute-start.21 = (bf16[48,4096]{1,0:T(8,128)(2,1)S(1)}, bf16[48,4096]{1,0:T(8,128)(2,1)S(1)}, u32[]{:S(2)}, u32[]{:S(2)}) collective-permute-start(bf16[48,4096]{1,0:T(8,128)(2,1)S(1)} %join_rows.3.refs_0_), channel_id=1, source_target_pairs={{0,8},{8,0},{16,24},{24,16},{1,9},{9,1},{17,25},{25,17},{2,10},{10... | collective-permute-start | bytes 1179656 | tf_op jit(solution)/shard_map/ppermute | solution.py:399
  140.7 9.1 %collective-permute-start.32 = (bf16[48,4096]{1,0:T(8,128)(2,1)S(1)}, bf16[48,4096]{1,0:T(8,128)(2,1)S(1)}, u32[]{:S(2)}, u32[]{:S(2)}) collective-permute-start(bf16[48,4096]{1,0:T(8,128)(2,1)S(1)} %collective-permute-done.28.refs_11_), channel_id=1, source_target_pairs={{0,8},{8,0},{16,24},{24,16},{1,9},{9,1},{17,25},{25,17},{2,10},{10... | collective-permute-start | bytes 1179656 | tf_op jit(solution)/shard_map/ppermute | solution.py:399
  148.0 1.8 %collective-permute-start.29 = (bf16[48,4096]{1,0:T(8,128)(2,1)S(1)}, bf16[48,4096]{1,0:T(8,128)(2,1)S(1)}, u32[]{:S(2)}, u32[]{:S(2)}) collective-permute-start(bf16[48,4096]{1,0:T(8,128)(2,1)S(1)} %collective-permute-done.25.refs_8_), channel_id=1, source_target_pairs={{0,8},{8,0},{16,24},{24,16},{1,9},{9,1},{17,25},{25,17},{2,10},{10... | collective-permute-start | bytes 1179656 | tf_op jit(solution)/shard_map/ppermute | solution.py:399

commit v2 on v1

--- a/solution.py
+++ b/solution.py
@@ -11,6 +11,7 @@
 NGROUP = 8
 KINDS = 3
 CAP = 24
+TOWER, DP = "tower", "dp"
 BF16 = jnp.bfloat16
 F32 = jnp.float32
 I32 = jnp.int32
@@ -181,7 +182,7 @@
 
 
 def column_pieces(dp_idx, blocks):
-    pieces = lax.axis_size("dp")
+    pieces = lax.axis_size(DP)
     width = blocks[0].shape[1]
     rows = len(blocks) * CAP
     whole = pl.BlockSpec(memory_space=pltpu.VMEM)
@@ -245,7 +246,6 @@
                 2 * slots * features * width, 2 * (features * width + 2 * slots * width)
             ),
             compiler_params=grant(24),
-            name="token_grad",
         )(dp_idx, *flat, *[weight] * pieces)
     )
 
@@ -298,7 +298,6 @@
         scratch_shapes=[pltpu.VMEM((rows, width), BF16)],
         cost_estimate=cost(2 * rows * tokens * width, 2 * (tokens + rows) * width),
         compiler_params=grant(12),
-        name="combine_first",
     )(one_hot, *blocks)
 
 
@@ -390,7 +389,6 @@
             2 * rows * features * columns, 2 * (rows * (features + columns) + features * columns)
         ),
         compiler_params=grant(20),
-        name="weight_grad",
     )(*attn_parts, *cot_parts)
 
 
@@ -405,30 +403,30 @@
         pairs = [(t, target_of(t, k)) for t in range(NGROUP)]
         if back:
             pairs = [(target, source) for source, target in pairs]
-        got.append(lax.ppermute(blocks[k], "tower", pairs))
+        got.append(lax.ppermute(blocks[k], TOWER, pairs))
     return got
 
 
 def gather_flips(value):
     parts = {0: value}
-    flip = lax.axis_size("dp") // 2
+    flip = lax.axis_size(DP) // 2
     while flip:
         for known in list(parts):
-            parts[known ^ flip] = flip_over("dp", parts[known], flip)
+            parts[known ^ flip] = flip_over(DP, parts[known], flip)
         flip //= 2
     return parts
 
 
-COT_PARTS = {"cot_early": (0, 1, 2, 3), "cot_late": (4, 5, 6, 7)}
-ATTN_PARTS = {"attn_a": (0, 1), "attn_b": (2,), "attn_c": (3, 4, 5), "attn_d": (6, 7)}
+COT_PARTS = {"ce": (0, 1, 2, 3), "cl": (4, 5, 6, 7)}
+ATTN_PARTS = {"aa": (0, 1), "ab": (2,), "ac": (3, 4, 5), "ad": (6, 7)}
 LAST = (6, 7)
-FIRST = (2, 3)
+FIRST = (2,)
 
 
 def small_towers(attn_out, out_cot, modality, group_modality, o_weight):
-    tower_idx = lax.axis_index("tower").astype(I32)
-    dp_idx = lax.axis_index("dp").astype(I32).reshape(1)
-    dp_count = lax.axis_size("dp")
+    tower_idx = lax.axis_index(TOWER).astype(I32)
+    dp_idx = lax.axis_index(DP).astype(I32).reshape(1)
+    dp_count = lax.axis_size(DP)
 
     every = tuple(range(NGROUP))
     rest = tuple(k for k in every if k not in FIRST)
@@ -444,7 +442,7 @@
         pieces = column_pieces(dp_idx, [cot_got[k] for k in blocks])
         cot_pieces.append(pieces)
         cot_moved.append(
-            [flip_over("dp", piece, flip) if flip else piece for flip, piece in enumerate(pieces)]
+            [flip_over(DP, piece, flip) if flip else piece for flip, piece in enumerate(pieces)]
         )
     cot_parts = [moved[flip] for flip in range(dp_count) for moved in cot_moved]
     grads = token_grad(dp_idx, cot_pieces, o_weight)
@@ -461,10 +459,10 @@
 
 
 def large_towers(attn_out, out_cot, modality, group_modality, o_weight):
-    tower_idx = lax.axis_index("tower").astype(I32)
-    tower_count = lax.axis_size("tower")
-    dp_idx = lax.axis_index("dp")
-    dp_count = lax.axis_size("dp")
+    tower_idx = lax.axis_index(TOWER).astype(I32)
+    tower_count = lax.axis_size(TOWER)
+    dp_idx = lax.axis_index(DP)
+    dp_count = lax.axis_size(DP)
     group_size = tower_count // NGROUP
     piece_rows, width = o_weight.shape
     tokens = attn_out.shape[0]
@@ -484,7 +482,7 @@
     one_hot = (place[None, :] == jnp.arange(NGROUP * CAP, dtype=I32)[:, None]).astype(BF16)
 
     def swap(value):
-        return lax.all_to_all(value, "tower", split_axis=0, concat_axis=0, tiled=True)
+        return lax.all_to_all(value, TOWER, split_axis=0, concat_axis=0, tiled=True)
 
     cot_group = jnp.dot(one_hot, out_cot, preferred_element_type=F32).astype(BF16)
     attn_group = jnp.dot(one_hot, attn_out, preferred_element_type=F32).astype(BF16)
@@ -513,13 +511,13 @@
     cot_parts = []
     for flip in range(dp_count):
         part = lax.dynamic_slice_in_dim(cot_rows, (dp_idx ^ flip) * piece_cols, piece_cols, 1)
-        cot_parts.append(flip_over("dp", part, flip) if flip else part)
+        cot_parts.append(flip_over(DP, part, flip) if flip else part)
     attn_parts = gather_flips(attn_rows)
     return attn_grad, weight_grad_of([attn_parts[flip] for flip in range(dp_count)], cot_parts)
 
 
 def per_device(*args):
-    if lax.axis_size("tower") == NGROUP:
+    if lax.axis_size(TOWER) == NGROUP:
         return small_towers(*args)
     return large_towers(*args)
 
@@ -529,12 +527,12 @@
         per_device,
         mesh=mesh,
         in_specs=(
-            P(("dp", "tower"), None),
-            P(("dp", "tower"), None),
-            P(("dp", "tower")),
+            P((DP, TOWER), None),
+            P((DP, TOWER), None),
+            P((DP, TOWER)),
             P(),
-            P("tower", None),
+            P(TOWER, None),
         ),
-        out_specs=(P(("dp", "tower"), None), P("tower", "dp")),
+        out_specs=(P((DP, TOWER), None), P(TOWER, DP)),
         check_vma=False,
     )

time: 161 us -> 161 us (level)
  transfers between devices with their start and end apart: 39 -> 39, of which waited for: 12 -> 13; matrix products, arithmetic and copies ran while one was open for 0% -> 0% of each run, Pallas kernels for 16% -> 16%
where the time goes in v2:
time: 161 us
  waiting for transfers between devices  76.7 us (48%)
  starting transfers between devices  45.4 us (28%)
  Pallas kernels  38.2 us (24%)
    ppermute x21, waiting for transfers between devices, swap_blocks(): got.append(lax.ppermute(blocks[k], TOWER, pairs))  64.1 us
    ppermute x21, starting transfers between devices, swap_blocks(): got.append(lax.ppermute(blocks[k], TOWER, pairs))  34.7 us
    pallas_call x1, Pallas kernels, token_grad(): pl.pallas_call(functools.partial(token_grad_kernel, pieces, len(cot_piece...  17.4 us
    ppermute x18, waiting for transfers between devices, flip_over(): return lax.ppermute(value, axis, [(i, i ^ flip) for i in range(size)])  12.6 us
    ppermute x18, starting transfers between devices, flip_over(): return lax.ppermute(value, axis, [(i, i ^ flip) for i in range(size)])  10.8 us
    pallas_call x1, Pallas kernels, weight_grad_of(): pl.pallas_call(functools.partial(weight_grad_kernel, len(attn_parts), len...  10.5 us
    pallas_call x2, Pallas kernels, dispatch_next(): pl.pallas_call(functools.partial(dispatch_kernel, blocks), grid=(width //...  6.57 us
  transfers between devices with their start and end apart: 39, of which 13 were waited for; matrix products, arithmetic and copies ran while one was open for 0% of the time, Pallas kernels for 16%

profile of v2, /device:TPU:0, one launch (start us, length us, event | category | flops | bytes accessed | tf_op | source)
XLA Modules:
  0.0 161.2 jit_solution(12640101279201284224)
XLA Ops:
  0.6 1.9 %dispatch_cot.1 = (bf16[192,128]{1,0:T(8,128)(2,1)S(1)}, bf16[24,4096]{1,0:T(8,128)(2,1)S(1)}) custom-call(s32[1]{0:T(128)} %bitcast.tower_ref, s32[8]{0:T(128)} %kinds_hbm.1, s32[1,128]{1,0:T(1,128)} %bitcast.3, bf16[128,4096]{1,0:T(8,128)(2,1)} %rows_ref.2), custom_call_target="tpu_custom_call" | custom-call | flops 201326592 | bytes 2621440 | tf_op jit(solution)/shard_map/dispatch_cot/pallas_call | solution.py:136
  2.5 3.1 %collective-permute-start.1 = (bf16[24,4096]{1,0:T(8,128)(2,1)S(1)}, bf16[24,4096]{1,0:T(8,128)(2,1)S(1)}, u32[]{:S(2)}, u32[]{:S(2)}) collective-permute-start(bf16[24,4096]{1,0:T(8,128)(2,1)S(1)} %get-tuple-element.38), channel_id=1, source_target_pairs={{0,2},{1,3},{2,4},{3,5},{4,6},{5,7},{6,0},{7,1},{8,10},{9,11},{10,... | collective-permute-start | bytes 589832 | tf_op jit(solution)/shard_map/ppermute | solution.py:406
  5.6 2.8 %shard_map.68 = (bf16[24,4096]{1,0:T(8,128)(2,1)S(1)}, bf16[24,4096]{1,0:T(8,128)(2,1)S(1)}, bf16[24,4096]{1,0:T(8,128)(2,1)S(1)}, bf16[24,4096]{1,0:T(8,128)(2,...) custom-call(bf16[192,128]{1,0:T(8,128)(2,1)S(1)} %get-tuple-element.35.one_hot_ref,, ...), custom_call_target="tpu_custom_call" | custom-call | flops 201326592 | bytes 2621440 | tf_op jit(solution)/shard_map/pallas_call | solution.py:160
  8.4 1.6 collective-permute-start
  10.0 1.6 collective-permute-start.2
  11.5 2.2 %collective-permute-start.3 = (bf16[24,4096]{1,0:T(8,128)(2,1)S(1)}, bf16[24,4096]{1,0:T(8,128)(2,1)S(1)}, u32[]{:S(2)}, u32[]{:S(2)}) collective-permute-start(bf16[24,4096]{1,0:T(8,128)(2,1)S(1)} %get-tuple-element.44), channel_id=1, source_target_pairs={{0,6},{1,7},{2,0},{3,1},{4,2},{5,3},{6,4},{7,5},{8,14},{9,15},{10,... | collective-permute-start | bytes 589832 | tf_op jit(solution)/shard_map/ppermute | solution.py:406
  13.8 1.4 collective-permute-start.4
  15.1 3.8 %shard_map.71 = (bf16[24,4096]{1,0:T(8,128)(2,1)}, bf16[24,4096]{1,0:T(8,128)(2,1)}, bf16[24,4096]{1,0:T(8,128)(2,1)}, bf16[24,4096]{1,0:T(8,128)(2,1)}, bf16[24...) custom-call(bf16[192,128]{1,0:T(8,128)(2,1)} %copy-done, ...), custom_call_target="tpu_custom_call" | custom-call | flops 201326592 | bytes 2621440 | tf_op jit(solution)/shard_map/pallas_call | solution.py:160
  18.9 0.9 collective-permute-start.5
  19.8 0.0 collective-permute-done.refs_1_
  19.8 3.5 %collective-permute-start.6 = (bf16[24,4096]{1,0:T(8,128)(2,1)S(1)}, bf16[24,4096]{1,0:T(8,128)(2,1)S(1)}, u32[]{:S(2)}, u32[]{:S(2)}) collective-permute-start(bf16[24,4096]{1,0:T(8,128)(2,1)S(1)} %get-tuple-element.47), channel_id=1, source_target_pairs={{0,5},{1,4},{2,7},{3,6},{4,1},{5,0},{6,3},{7,2},{8,13},{9,12},{10,... | collective-permute-start | bytes 589832 | tf_op jit(solution)/shard_map/ppermute | solution.py:406
  23.3 0.1 collective-permute-start.14
  23.4 0.0 collective-permute-done.3.refs_0_
  23.4 1.6 collective-permute-start.15
  25.0 1.8 %collective-permute-done.4.refs_1_ = bf16[24,4096]{1,0:T(8,128)(2,1)S(1)} collective-permute-done((bf16[24,4096]{1,0:T(8,128)(2,1)S(1)}, bf16[24,4096]{1,0:T(8,128)(2,1)S(1)}, u32[]{:S(2)}, u32[]{:S(2)}) %collective-permute-start.4) | collective-permute-done | bytes 196640 | tf_op jit(solution)/shard_map/ppermute | solution.py:406
  26.8 10.1 %collective-permute-start.16 = (bf16[24,4096]{1,0:T(8,128)(2,1)}, bf16[24,4096]{1,0:T(8,128)(2,1)S(1)}, u32[]{:S(2)}, u32[]{:S(2)}) collective-permute-start(bf16[24,4096]{1,0:T(8,128)(2,1)} %get-tuple-element.63), channel_id=1, source_target_pairs={{0,3},{1,2},{2,5},{3,4},{4,7},{5,6},{6,1},{7,0},{8,11},{9,10},{10,... | collective-permute-start | bytes 589832 | tf_op jit(solution)/shard_map/ppermute | solution.py:406
  36.9 0.1 column_pieces.2
  37.0 10.4 %collective-permute-done.5.refs_2_ = bf16[24,4096]{1,0:T(8,128)(2,1)S(1)} collective-permute-done((bf16[24,4096]{1,0:T(8,128)(2,1)S(1)}, bf16[24,4096]{1,0:T(8,128)(2,1)S(1)}, u32[]{:S(2)}, u32[]{:S(2)}) %collective-permute-start.5) | collective-permute-done | bytes 196640 | tf_op jit(solution)/shard_map/ppermute | solution.py:406
  47.4 5.2 %collective-permute-done.6.refs_3_ = bf16[24,4096]{1,0:T(8,128)(2,1)S(1)} collective-permute-done((bf16[24,4096]{1,0:T(8,128)(2,1)S(1)}, bf16[24,4096]{1,0:T(8,128)(2,1)S(1)}, u32[]{:S(2)}, u32[]{:S(2)}) %collective-permute-start.6) | collective-permute-done | bytes 196640 | tf_op jit(solution)/shard_map/ppermute | solution.py:406
  52.6 0.0 collective-permute-start.18
  52.6 0.0 collective-permute-done.15.refs_1_
  52.6 2.9 %collective-permute-start.20 = (bf16[24,4096]{1,0:T(8,128)(2,1)}, bf16[24,4096]{1,0:T(8,128)(2,1)S(1)}, u32[]{:S(2)}, u32[]{:S(2)}) collective-permute-start(bf16[24,4096]{1,0:T(8,128)(2,1)} %get-tuple-element.67), channel_id=1, source_target_pairs={{0,5},{1,4},{2,7},{3,6},{4,1},{5,0},{6,3},{7,2},{8,13},{9,12},{10,... | collective-permute-start | bytes 589832 | tf_op jit(solution)/shard_map/ppermute | solution.py:406
  55.5 0.0 collective-permute-done.16.refs_0_
  55.5 0.0 collective-permute-start.33
  55.5 0.1 column_pieces.3
  55.5 0.3 collective-permute-done.17.refs_1_
  55.8 1.5 collective-permute-start.35
  57.3 3.6 %collective-permute-done.18.refs_2_ = bf16[24,4096]{1,0:T(8,128)(2,1)S(1)} collective-permute-done((bf16[24,4096]{1,0:T(8,128)(2,1)}, bf16[24,4096]{1,0:T(8,128)(2,1)S(1)}, u32[]{:S(2)}, u32[]{:S(2)}) %collective-permute-start.18) | collective-permute-done | bytes 196640 | tf_op jit(solution)/shard_map/ppermute | solution.py:406
  60.9 0.7 collective-permute-start.37
  61.6 11.1 %collective-permute-done.19.refs_0_ = bf16[24,4096]{1,0:T(8,128)(2,1)S(1)} collective-permute-done((bf16[24,4096]{1,0:T(8,128)(2,1)}, bf16[24,4096]{1,0:T(8,128)(2,1)S(1)}, u32[]{:S(2)}, u32[]{:S(2)}) %collective-permute-start.19) | collective-permute-done | bytes 196640 | tf_op jit(solution)/shard_map/ppermute | solution.py:406
  72.7 5.1 %collective-permute-done.20.refs_1_ = bf16[24,4096]{1,0:T(8,128)(2,1)S(1)} collective-permute-done((bf16[24,4096]{1,0:T(8,128)(2,1)}, bf16[24,4096]{1,0:T(8,128)(2,1)S(1)}, u32[]{:S(2)}, u32[]{:S(2)}) %collective-permute-start.20) | collective-permute-done | bytes 196640 | tf_op jit(solution)/shard_map/ppermute | solution.py:406
  77.8 1.5 collective-permute-start.36
  79.3 0.0 collective-permute-done.33.refs_18_
  79.3 17.4 %shard_map.69 = (bf16[24,4096]{1,0:T(8,128)(2,1)S(1)}, bf16[24,4096]{1,0:T(8,128)(2,1)S(1)}, bf16[24,4096]{1,0:T(8,128)(2,1)S(1)}, bf16[24,4096]{1,0:T(8,128)(2,...) custom-call(s32[1]{0:T(128)} %bitcast.2.dp_ref, ...), custom_call_target="tpu_custom_call" | custom-call | flops 6442450944 | bytes 36700160 | tf_op jit(solution)/shard_map/pallas_call | solution.py:234
  96.7 0.6 collective-permute-start.7
  97.3 1.8 %collective-permute-start.8 = (bf16[24,4096]{1,0:T(8,128)(2,1)S(1)}, bf16[24,4096]{1,0:T(8,128)(2,1)S(1)}, u32[]{:S(2)}, u32[]{:S(2)}) collective-permute-start(bf16[24,4096]{1,0:T(8,128)(2,1)S(1)} %get-tuple-element.54), channel_id=1, source_target_pairs={{2,0},{3,1},{4,2},{5,3},{6,4},{7,5},{0,6},{1,7},{10,8},{11,9},{12,... | collective-permute-start | bytes 589832 | tf_op jit(solution)/shard_map/ppermute | solution.py:406
  99.1 1.0 collective-permute-start.9
  100.1 0.0 collective-permute-done.36.refs_21_
  100.1 2.0 %collective-permute-start.10 = (bf16[24,4096]{1,0:T(8,128)(2,1)S(1)}, bf16[24,4096]{1,0:T(8,128)(2,1)S(1)}, u32[]{:S(2)}, u32[]{:S(2)}) collective-permute-start(bf16[24,4096]{1,0:T(8,128)(2,1)S(1)} %get-tuple-element.56), channel_id=1, source_target_pairs={{6,0},{7,1},{0,2},{1,3},{2,4},{3,5},{4,6},{5,7},{14,8},{15,9},{8,1... | collective-permute-start | bytes 589832 | tf_op jit(solution)/shard_map/ppermute | solution.py:406
  102.0 0.0 collective-permute-done.38.refs_23_
  102.0 0.2 collective-permute-start.11
  102.3 1.8 %collective-permute-done.7.refs_1_ = bf16[24,4096]{1,0:T(8,128)(2,1)S(1)} collective-permute-done((bf16[24,4096]{1,0:T(8,128)(2,1)S(1)}, bf16[24,4096]{1,0:T(8,128)(2,1)S(1)}, u32[]{:S(2)}, u32[]{:S(2)}) %collective-permute-start.7) | collective-permute-done | bytes 196640 | tf_op jit(solution)/shard_map/ppermute | solution.py:406
  104.1 1.5 collective-permute-start.27
  105.7 0.0 collective-permute-done.8.refs_2_
  105.7 0.3 collective-permute-start.12
  105.9 12.8 %collective-permute-done.9.refs_3_ = bf16[24,4096]{1,0:T(8,128)(2,1)S(1)} collective-permute-done((bf16[24,4096]{1,0:T(8,128)(2,1)S(1)}, bf16[24,4096]{1,0:T(8,128)(2,1)S(1)}, u32[]{:S(2)}, u32[]{:S(2)}) %collective-permute-start.9) | collective-permute-done | bytes 196640 | tf_op jit(solution)/shard_map/ppermute | solution.py:406
  118.7 1.8 %collective-permute-start.26 = (bf16[24,4096]{1,0:T(8,128)(2,1)S(1)}, bf16[24,4096]{1,0:T(8,128)(2,1)S(1)}, u32[]{:S(2)}, u32[]{:S(2)}) collective-permute-start(bf16[24,4096]{1,0:T(8,128)(2,1)S(1)} %collective-permute-done.15.refs_1_), channel_id=1, source_target_pairs={{0,16},{8,24},{16,0},{24,8},{1,17},{9,25},{17,1},{25,9},{2,18},{10... | collective-permute-start | bytes 589832 | tf_op jit(solution)/shard_map/ppermute | solution.py:397
  120.5 0.0 collective-permute-done.10.refs_4_
  120.5 0.0 collective-permute-start.13
  120.5 0.0 collective-permute-done.11.refs_5_
  120.5 0.1 collective-permute-start.22
  120.7 9.1 %collective-permute-done.12.refs_0_ = bf16[24,4096]{1,0:T(8,128)(2,1)S(1)} collective-permute-done((bf16[24,4096]{1,0:T(8,128)(2,1)S(1)}, bf16[24,4096]{1,0:T(8,128)(2,1)S(1)}, u32[]{:S(2)}, u32[]{:S(2)}) %collective-permute-start.12) | collective-permute-done | bytes 196640 | tf_op jit(solution)/shard_map/ppermute | solution.py:406
  129.8 1.4 collective-permute-start.28
  131.2 0.0 collective-permute-done.26.refs_9_
  131.2 2.9 %collective-permute-done.13.refs_1_ = bf16[24,4096]{1,0:T(8,128)(2,1)S(1)} collective-permute-done((bf16[24,4096]{1,0:T(8,128)(2,1)S(1)}, bf16[24,4096]{1,0:T(8,128)(2,1)S(1)}, u32[]{:S(2)}, u32[]{:S(2)}) %collective-permute-start.13) | collective-permute-done | bytes 196640 | tf_op jit(solution)/shard_map/ppermute | solution.py:406
  134.1 1.2 collective-permute-start.25
  135.3 0.2 collective-permute-start.23
  135.5 0.3 collective-permute-start.31
  135.8 6.0 %collective-permute-done.28.refs_11_ = bf16[48,4096]{1,0:T(8,128)(2,1)S(1)} collective-permute-done((bf16[48,4096]{1,0:T(8,128)(2,1)S(1)}, bf16[48,4096]{1,0:T(8,128)(2,1)S(1)}, u32[]{:S(2)}, u32[]{:S(2)}) %collective-permute-start.28) | collective-permute-done | bytes 393248 | tf_op jit(solution)/shard_map/ppermute | solution.py:397
  141.8 0.5 collective-permute-start.32
  142.3 6.6 %collective-permute-done.25.refs_8_ = bf16[48,4096]{1,0:T(8,128)(2,1)S(1)} collective-permute-done((bf16[48,4096]{1,0:T(8,128)(2,1)S(1)}, bf16[48,4096]{1,0:T(8,128)(2,1)S(1)}, u32[]{:S(2)}, u32[]{:S(2)}) %collective-permute-start.25) | collective-permute-done | bytes 393248 | tf_op jit(solution)/shard_map/ppermute | solution.py:397
  148.9 0.5 shard_map.70.partial_ref
  149.4 1.3 combine_last.1
  150.7 10.5 %shard_map.72 = bf16[4096,1024]{1,0:T(8,128)(2,1)} custom-call(bf16[48,4096]{1,0:T(8,128)(2,1)S(1)} %join_rows.3.refs_0_, bf16[24,4096]{1,0:T(8,128)(2,1)S(1)} %collective-permute-done.15.refs_1_, bf16[72,4096]{1,0:T(8,128)(2,1)S(1)} %join_rows.4.refs_2_, bf16[48,4096]{1,0:T(8,128)(2,1)S(1)} %join_rows.5.refs_3_, ...), custom_call_target="tpu_custom_call" | custom-call | flops 6442450944 | bytes 16252928 | tf_op jit(solution)/shard_map/pallas_call | solution.py:380
  (32 shorter events, 0.2 us)
Async XLA Ops:
  2.5 12.6 %copy-start = (bf16[192,128]{1,0:T(8,128)(2,1)}, bf16[192,128]{1,0:T(8,128)(2,1)S(1)}, u32[]{:S(2)}) copy-start(bf16[192,128]{1,0:T(8,128)(2,1)S(1)} %get-tuple-element.35.one_hot_ref) | copy-start | bytes 147460
  2.5 16.4 %collective-permute-start.1 = (bf16[24,4096]{1,0:T(8,128)(2,1)S(1)}, bf16[24,4096]{1,0:T(8,128)(2,1)S(1)}, u32[]{:S(2)}, u32[]{:S(2)}) collective-permute-start(bf16[24,4096]{1,0:T(8,128)(2,1)S(1)} %get-tuple-element.38), channel_id=1, source_target_pairs={{0,2},{1,3},{2,4},{3,5},{4,6},{5,7},{6,0},{7,1},{8,10},{9,11},{10,... | collective-permute-start | bytes 589832 | tf_op jit(solution)/shard_map/ppermute | solution.py:406
  8.4 11.4 %collective-permute-start = (bf16[24,4096]{1,0:T(8,128)(2,1)S(1)}, bf16[24,4096]{1,0:T(8,128)(2,1)S(1)}, u32[]{:S(2)}, u32[]{:S(2)}) collective-permute-start(bf16[24,4096]{1,0:T(8,128)(2,1)S(1)} %get-tuple-element.37), channel_id=1, source_target_pairs={{0,1},{1,0},{2,3},{3,2},{4,5},{5,4},{6,7},{7,6},{8,9},{9,8},{10,11... | collective-permute-start | bytes 589832 | tf_op jit(solution)/shard_map/ppermute | solution.py:406
  10.0 13.3 %collective-permute-start.2 = (bf16[24,4096]{1,0:T(8,128)(2,1)S(1)}, bf16[24,4096]{1,0:T(8,128)(2,1)S(1)}, u32[]{:S(2)}, u32[]{:S(2)}) collective-permute-start(bf16[24,4096]{1,0:T(8,128)(2,1)S(1)} %get-tuple-element.39), channel_id=1, source_target_pairs={{0,3},{1,2},{2,5},{3,4},{4,7},{5,6},{6,1},{7,0},{8,11},{9,10},{10,... | collective-permute-start | bytes 589832 | tf_op jit(solution)/shard_map/ppermute | solution.py:406
  11.5 11.9 %collective-permute-start.3 = (bf16[24,4096]{1,0:T(8,128)(2,1)S(1)}, bf16[24,4096]{1,0:T(8,128)(2,1)S(1)}, u32[]{:S(2)}, u32[]{:S(2)}) collective-permute-start(bf16[24,4096]{1,0:T(8,128)(2,1)S(1)} %get-tuple-element.44), channel_id=1, source_target_pairs={{0,6},{1,7},{2,0},{3,1},{4,2},{5,3},{6,4},{7,5},{8,14},{9,15},{10,... | collective-permute-start | bytes 589832 | tf_op jit(solution)/shard_map/ppermute | solution.py:406
  13.8 13.0 %collective-permute-start.4 = (bf16[24,4096]{1,0:T(8,128)(2,1)S(1)}, bf16[24,4096]{1,0:T(8,128)(2,1)S(1)}, u32[]{:S(2)}, u32[]{:S(2)}) collective-permute-start(bf16[24,4096]{1,0:T(8,128)(2,1)S(1)} %get-tuple-element.45), channel_id=1, source_target_pairs={{0,7},{1,6},{2,1},{3,0},{4,3},{5,2},{6,5},{7,4},{8,15},{9,14},{10,... | collective-permute-start | bytes 589832 | tf_op jit(solution)/shard_map/ppermute | solution.py:406
  18.9 28.5 %collective-permute-start.5 = (bf16[24,4096]{1,0:T(8,128)(2,1)S(1)}, bf16[24,4096]{1,0:T(8,128)(2,1)S(1)}, u32[]{:S(2)}, u32[]{:S(2)}) collective-permute-start(bf16[24,4096]{1,0:T(8,128)(2,1)S(1)} %get-tuple-element.46), channel_id=1, source_target_pairs={{0,4},{1,5},{2,6},{3,7},{4,0},{5,1},{6,2},{7,3},{8,12},{9,13},{10,... | collective-permute-start | bytes 589832 | tf_op jit(solution)/shard_map/ppermute | solution.py:406
  19.8 32.8 %collective-permute-start.6 = (bf16[24,4096]{1,0:T(8,128)(2,1)S(1)}, bf16[24,4096]{1,0:T(8,128)(2,1)S(1)}, u32[]{:S(2)}, u32[]{:S(2)}) collective-permute-start(bf16[24,4096]{1,0:T(8,128)(2,1)S(1)} %get-tuple-element.47), channel_id=1, source_target_pairs={{0,5},{1,4},{2,7},{3,6},{4,1},{5,0},{6,3},{7,2},{8,13},{9,12},{10,... | collective-permute-start | bytes 589832 | tf_op jit(solution)/shard_map/ppermute | solution.py:406
  23.3 29.3 %collective-permute-start.14 = (bf16[24,4096]{1,0:T(8,128)(2,1)}, bf16[24,4096]{1,0:T(8,128)(2,1)S(1)}, u32[]{:S(2)}, u32[]{:S(2)}) collective-permute-start(bf16[24,4096]{1,0:T(8,128)(2,1)} %get-tuple-element.61), channel_id=1, source_target_pairs={{0,1},{1,0},{2,3},{3,2},{4,5},{5,4},{6,7},{7,6},{8,9},{9,8},{10,11... | collective-permute-start | bytes 589832 | tf_op jit(solution)/shard_map/ppermute | solution.py:406
  23.4 29.2 %collective-permute-start.15 = (bf16[24,4096]{1,0:T(8,128)(2,1)}, bf16[24,4096]{1,0:T(8,128)(2,1)S(1)}, u32[]{:S(2)}, u32[]{:S(2)}) collective-permute-start(bf16[24,4096]{1,0:T(8,128)(2,1)} %get-tuple-element.62), channel_id=1, source_target_pairs={{0,2},{1,3},{2,4},{3,5},{4,6},{5,7},{6,0},{7,1},{8,10},{9,11},{10,... | collective-permute-start | bytes 589832 | tf_op jit(solution)/shard_map/ppermute | solution.py:406
  26.8 28.7 %collective-permute-start.16 = (bf16[24,4096]{1,0:T(8,128)(2,1)}, bf16[24,4096]{1,0:T(8,128)(2,1)S(1)}, u32[]{:S(2)}, u32[]{:S(2)}) collective-permute-start(bf16[24,4096]{1,0:T(8,128)(2,1)} %get-tuple-element.63), channel_id=1, source_target_pairs={{0,3},{1,2},{2,5},{3,4},{4,7},{5,6},{6,1},{7,0},{8,11},{9,10},{10,... | collective-permute-start | bytes 589832 | tf_op jit(solution)/shard_map/ppermute | solution.py:406
  47.4 8.4 %collective-permute-start.17 = (bf16[24,4096]{1,0:T(8,128)(2,1)}, bf16[24,4096]{1,0:T(8,128)(2,1)S(1)}, u32[]{:S(2)}, u32[]{:S(2)}) collective-permute-start(bf16[24,4096]{1,0:T(8,128)(2,1)} %get-tuple-element.64), channel_id=1, source_target_pairs={{0,6},{1,7},{2,0},{3,1},{4,2},{5,3},{6,4},{7,5},{8,14},{9,15},{10,... | collective-permute-start | bytes 589832 | tf_op jit(solution)/shard_map/ppermute | solution.py:406
  52.6 8.3 %collective-permute-start.18 = (bf16[24,4096]{1,0:T(8,128)(2,1)}, bf16[24,4096]{1,0:T(8,128)(2,1)S(1)}, u32[]{:S(2)}, u32[]{:S(2)}) collective-permute-start(bf16[24,4096]{1,0:T(8,128)(2,1)} %get-tuple-element.65), channel_id=1, source_target_pairs={{0,7},{1,6},{2,1},{3,0},{4,3},{5,2},{6,5},{7,4},{8,15},{9,14},{10,... | collective-permute-start | bytes 589832 | tf_op jit(solution)/shard_map/ppermute | solution.py:406
  52.6 20.1 %collective-permute-start.19 = (bf16[24,4096]{1,0:T(8,128)(2,1)}, bf16[24,4096]{1,0:T(8,128)(2,1)S(1)}, u32[]{:S(2)}, u32[]{:S(2)}) collective-permute-start(bf16[24,4096]{1,0:T(8,128)(2,1)} %get-tuple-element.66), channel_id=1, source_target_pairs={{0,4},{1,5},{2,6},{3,7},{4,0},{5,1},{6,2},{7,3},{8,12},{9,13},{10,... | collective-permute-start | bytes 589832 | tf_op jit(solution)/shard_map/ppermute | solution.py:406
  52.6 25.2 %collective-permute-start.20 = (bf16[24,4096]{1,0:T(8,128)(2,1)}, bf16[24,4096]{1,0:T(8,128)(2,1)S(1)}, u32[]{:S(2)}, u32[]{:S(2)}) collective-permute-start(bf16[24,4096]{1,0:T(8,128)(2,1)} %get-tuple-element.67), channel_id=1, source_target_pairs={{0,5},{1,4},{2,7},{3,6},{4,1},{5,0},{6,3},{7,2},{8,13},{9,12},{10,... | collective-permute-start | bytes 589832 | tf_op jit(solution)/shard_map/ppermute | solution.py:406
  55.5 23.8 %collective-permute-start.33 = (bf16[96,1024]{1,0:T(8,128)(2,1)S(1)}, bf16[96,1024]{1,0:T(8,128)(2,1)S(1)}, u32[]{:S(2)}, u32[]{:S(2)}) collective-permute-start(bf16[96,1024]{1,0:T(8,128)(2,1)S(1)} %get-tuple-element.41.refs_1_), channel_id=1, source_target_pairs={{0,8},{8,0},{16,24},{24,16},{1,9},{9,1},{17,25},{25,17},{2,10},{10... | collective-permute-start | bytes 589832 | tf_op jit(solution)/shard_map/ppermute | solution.py:397
  55.8 40.9 %collective-permute-start.35 = (bf16[96,1024]{1,0:T(8,128)(2,1)S(1)}, bf16[96,1024]{1,0:T(8,128)(2,1)S(1)}, u32[]{:S(2)}, u32[]{:S(2)}) collective-permute-start(bf16[96,1024]{1,0:T(8,128)(2,1)S(1)} %get-tuple-element.42.refs_2_), channel_id=1, source_target_pairs={{0,16},{8,24},{16,0},{24,8},{1,17},{9,25},{17,1},{25,9},{2,18},{10... | collective-permute-start | bytes 589832 | tf_op jit(solution)/shard_map/ppermute | solution.py:397
  60.9 36.4 %collective-permute-start.37 = (bf16[96,1024]{1,0:T(8,128)(2,1)S(1)}, bf16[96,1024]{1,0:T(8,128)(2,1)S(1)}, u32[]{:S(2)}, u32[]{:S(2)}) collective-permute-start(bf16[96,1024]{1,0:T(8,128)(2,1)S(1)} %get-tuple-element.43.refs_3_), channel_id=1, source_target_pairs={{0,24},{8,16},{16,8},{24,0},{1,25},{9,17},{17,9},{25,1},{2,26},{10... | collective-permute-start | bytes 589832 | tf_op jit(solution)/shard_map/ppermute | solution.py:397
  72.7 26.4 %collective-permute-start.34 = (bf16[96,1024]{1,0:T(8,128)(2,1)S(1)}, bf16[96,1024]{1,0:T(8,128)(2,1)S(1)}, u32[]{:S(2)}, u32[]{:S(2)}) collective-permute-start(bf16[96,1024]{1,0:T(8,128)(2,1)S(1)} %get-tuple-element.49.refs_5_), channel_id=1, source_target_pairs={{0,8},{8,0},{16,24},{24,16},{1,9},{9,1},{17,25},{25,17},{2,10},{10... | collective-permute-start | bytes 589832 | tf_op jit(solution)/shard_map/ppermute | solution.py:397
  77.8 22.3 %collective-permute-start.36 = (bf16[96,1024]{1,0:T(8,128)(2,1)S(1)}, bf16[96,1024]{1,0:T(8,128)(2,1)S(1)}, u32[]{:S(2)}, u32[]{:S(2)}) collective-permute-start(bf16[96,1024]{1,0:T(8,128)(2,1)S(1)} %get-tuple-element.50.refs_6_), channel_id=1, source_target_pairs={{0,16},{8,24},{16,0},{24,8},{1,17},{9,25},{17,1},{25,9},{2,18},{10... | collective-permute-start | bytes 589832 | tf_op jit(solution)/shard_map/ppermute | solution.py:397
  79.3 22.8 %collective-permute-start.38 = (bf16[96,1024]{1,0:T(8,128)(2,1)S(1)}, bf16[96,1024]{1,0:T(8,128)(2,1)S(1)}, u32[]{:S(2)}, u32[]{:S(2)}) collective-permute-start(bf16[96,1024]{1,0:T(8,128)(2,1)S(1)} %get-tuple-element.51.refs_7_), channel_id=1, source_target_pairs={{0,24},{8,16},{16,8},{24,0},{1,25},{9,17},{17,9},{25,1},{2,26},{10... | collective-permute-start | bytes 589832 | tf_op jit(solution)/shard_map/ppermute | solution.py:397
  79.3 41.3 %copy-start.2 = (bf16[24,4096]{1,0:T(8,128)(2,1)S(1)}, bf16[24,4096]{1,0:T(8,128)(2,1)}, u32[]{:S(2)}) copy-start(bf16[24,4096]{1,0:T(8,128)(2,1)} %get-tuple-element.60.refs_0_) | copy-start | bytes 589828
  79.3 69.6 %copy-start.1 = (bf16[192,128]{1,0:T(8,128)(2,1)S(1)}, bf16[192,128]{1,0:T(8,128)(2,1)}, u32[]{:S(2)}) copy-start(bf16[192,128]{1,0:T(8,128)(2,1)} %copy-done) | copy-start | bytes 147460
  96.7 7.4 %collective-permute-start.7 = (bf16[24,4096]{1,0:T(8,128)(2,1)S(1)}, bf16[24,4096]{1,0:T(8,128)(2,1)S(1)}, u32[]{:S(2)}, u32[]{:S(2)}) collective-permute-start(bf16[24,4096]{1,0:T(8,128)(2,1)S(1)} %get-tuple-element.53), channel_id=1, source_target_pairs={{1,0},{0,1},{3,2},{2,3},{5,4},{4,5},{7,6},{6,7},{9,8},{8,9},{11,10... | collective-permute-start | bytes 589832 | tf_op jit(solution)/shard_map/ppermute | solution.py:406
  97.3 8.4 %collective-permute-start.8 = (bf16[24,4096]{1,0:T(8,128)(2,1)S(1)}, bf16[24,4096]{1,0:T(8,128)(2,1)S(1)}, u32[]{:S(2)}, u32[]{:S(2)}) collective-permute-start(bf16[24,4096]{1,0:T(8,128)(2,1)S(1)} %get-tuple-element.54), channel_id=1, source_target_pairs={{2,0},{3,1},{4,2},{5,3},{6,4},{7,5},{0,6},{1,7},{10,8},{11,9},{12,... | collective-permute-start | bytes 589832 | tf_op jit(solution)/shard_map/ppermute | solution.py:406
  99.1 19.7 %collective-permute-start.9 = (bf16[24,4096]{1,0:T(8,128)(2,1)S(1)}, bf16[24,4096]{1,0:T(8,128)(2,1)S(1)}, u32[]{:S(2)}, u32[]{:S(2)}) collective-permute-start(bf16[24,4096]{1,0:T(8,128)(2,1)S(1)} %get-tuple-element.55), channel_id=1, source_target_pairs={{3,0},{2,1},{5,2},{4,3},{7,4},{6,5},{1,6},{0,7},{11,8},{10,9},{13,... | collective-permute-start | bytes 589832 | tf_op jit(solution)/shard_map/ppermute | solution.py:406
  100.1 20.5 %collective-permute-start.10 = (bf16[24,4096]{1,0:T(8,128)(2,1)S(1)}, bf16[24,4096]{1,0:T(8,128)(2,1)S(1)}, u32[]{:S(2)}, u32[]{:S(2)}) collective-permute-start(bf16[24,4096]{1,0:T(8,128)(2,1)S(1)} %get-tuple-element.56), channel_id=1, source_target_pairs={{6,0},{7,1},{0,2},{1,3},{2,4},{3,5},{4,6},{5,7},{14,8},{15,9},{8,1... | collective-permute-start | bytes 589832 | tf_op jit(solution)/shard_map/ppermute | solution.py:406
  102.0 18.5 %collective-permute-start.11 = (bf16[24,4096]{1,0:T(8,128)(2,1)S(1)}, bf16[24,4096]{1,0:T(8,128)(2,1)S(1)}, u32[]{:S(2)}, u32[]{:S(2)}) collective-permute-start(bf16[24,4096]{1,0:T(8,128)(2,1)S(1)} %get-tuple-element.57), channel_id=1, source_target_pairs={{7,0},{6,1},{1,2},{0,3},{3,4},{2,5},{5,6},{4,7},{15,8},{14,9},{9,1... | collective-permute-start | bytes 589832 | tf_op jit(solution)/shard_map/ppermute | solution.py:406
  104.1 31.4 %collective-permute-start.27 = (bf16[72,4096]{1,0:T(8,128)(2,1)S(1)}, bf16[72,4096]{1,0:T(8,128)(2,1)S(1)}, u32[]{:S(2)}, u32[]{:S(2)}) collective-permute-start(bf16[72,4096]{1,0:T(8,128)(2,1)S(1)} %join_rows.4.refs_2_), channel_id=1, source_target_pairs={{0,16},{8,24},{16,0},{24,8},{1,17},{9,25},{17,1},{25,9},{2,18},{10... | collective-permute-start | bytes 1769480 | tf_op jit(solution)/shard_map/ppermute | solution.py:397
  105.7 24.1 %collective-permute-start.12 = (bf16[24,4096]{1,0:T(8,128)(2,1)S(1)}, bf16[24,4096]{1,0:T(8,128)(2,1)S(1)}, u32[]{:S(2)}, u32[]{:S(2)}) collective-permute-start(bf16[24,4096]{1,0:T(8,128)(2,1)S(1)} %get-tuple-element.58), channel_id=1, source_target_pairs={{4,0},{5,1},{6,2},{7,3},{0,4},{1,5},{2,6},{3,7},{12,8},{13,9},{14,... | collective-permute-start | bytes 589832 | tf_op jit(solution)/shard_map/ppermute | solution.py:406
  118.7 12.5 %collective-permute-start.26 = (bf16[24,4096]{1,0:T(8,128)(2,1)S(1)}, bf16[24,4096]{1,0:T(8,128)(2,1)S(1)}, u32[]{:S(2)}, u32[]{:S(2)}) collective-permute-start(bf16[24,4096]{1,0:T(8,128)(2,1)S(1)} %collective-permute-done.15.refs_1_), channel_id=1, source_target_pairs={{0,16},{8,24},{16,0},{24,8},{1,17},{9,25},{17,1},{25,9},{2,18},{10... | collective-permute-start | bytes 589832 | tf_op jit(solution)/shard_map/ppermute | solution.py:397
  120.5 13.5 %collective-permute-start.13 = (bf16[24,4096]{1,0:T(8,128)(2,1)S(1)}, bf16[24,4096]{1,0:T(8,128)(2,1)S(1)}, u32[]{:S(2)}, u32[]{:S(2)}) collective-permute-start(bf16[24,4096]{1,0:T(8,128)(2,1)S(1)} %get-tuple-element.59), channel_id=1, source_target_pairs={{5,0},{4,1},{7,2},{6,3},{1,4},{0,5},{3,6},{2,7},{13,8},{12,9},{15,... | collective-permute-start | bytes 589832 | tf_op jit(solution)/shard_map/ppermute | solution.py:406
  120.5 13.5 %collective-permute-start.22 = (bf16[24,4096]{1,0:T(8,128)(2,1)S(1)}, bf16[24,4096]{1,0:T(8,128)(2,1)S(1)}, u32[]{:S(2)}, u32[]{:S(2)}) collective-permute-start(bf16[24,4096]{1,0:T(8,128)(2,1)S(1)} %collective-permute-done.15.refs_1_), channel_id=1, source_target_pairs={{0,8},{8,0},{16,24},{24,16},{1,9},{9,1},{17,25},{25,17},{2,10},{10... | collective-permute-start | bytes 589832 | tf_op jit(solution)/shard_map/ppermute | solution.py:397
  129.8 12.0 %collective-permute-start.28 = (bf16[48,4096]{1,0:T(8,128)(2,1)S(1)}, bf16[48,4096]{1,0:T(8,128)(2,1)S(1)}, u32[]{:S(2)}, u32[]{:S(2)}) collective-permute-start(bf16[48,4096]{1,0:T(8,128)(2,1)S(1)} %join_rows.5.refs_3_), channel_id=1, source_target_pairs={{0,16},{8,24},{16,0},{24,8},{1,17},{9,25},{17,1},{25,9},{2,18},{10... | collective-permute-start | bytes 1179656 | tf_op jit(solution)/shard_map/ppermute | solution.py:397
  131.2 4.1 %collective-permute-start.30 = (bf16[24,4096]{1,0:T(8,128)(2,1)S(1)}, bf16[24,4096]{1,0:T(8,128)(2,1)S(1)}, u32[]{:S(2)}, u32[]{:S(2)}) collective-permute-start(bf16[24,4096]{1,0:T(8,128)(2,1)S(1)} %collective-permute-done.26.refs_9_), channel_id=1, source_target_pairs={{0,8},{8,0},{16,24},{24,16},{1,9},{9,1},{17,25},{25,17},{2,10},{10... | collective-permute-start | bytes 589832 | tf_op jit(solution)/shard_map/ppermute | solution.py:397
  134.0 7.7 %collective-permute-start.24 = (bf16[48,4096]{1,0:T(8,128)(2,1)S(1)}, bf16[48,4096]{1,0:T(8,128)(2,1)S(1)}, u32[]{:S(2)}, u32[]{:S(2)}) collective-permute-start(bf16[48,4096]{1,0:T(8,128)(2,1)S(1)} %join_rows.5.refs_3_), channel_id=1, source_target_pairs={{0,8},{8,0},{16,24},{24,16},{1,9},{9,1},{17,25},{25,17},{2,10},{10... | collective-permute-start | bytes 1179656 | tf_op jit(solution)/shard_map/ppermute | solution.py:397
  134.1 14.9 %collective-permute-start.25 = (bf16[48,4096]{1,0:T(8,128)(2,1)S(1)}, bf16[48,4096]{1,0:T(8,128)(2,1)S(1)}, u32[]{:S(2)}, u32[]{:S(2)}) collective-permute-start(bf16[48,4096]{1,0:T(8,128)(2,1)S(1)} %join_rows.3.refs_0_), channel_id=1, source_target_pairs={{0,16},{8,24},{16,0},{24,8},{1,17},{9,25},{17,1},{25,9},{2,18},{10... | collective-permute-start | bytes 1179656 | tf_op jit(solution)/shard_map/ppermute | solution.py:397
  135.3 15.4 %collective-permute-start.23 = (bf16[72,4096]{1,0:T(8,128)(2,1)S(1)}, bf16[72,4096]{1,0:T(8,128)(2,1)S(1)}, u32[]{:S(2)}, u32[]{:S(2)}) collective-permute-start(bf16[72,4096]{1,0:T(8,128)(2,1)S(1)} %join_rows.4.refs_2_), channel_id=1, source_target_pairs={{0,8},{8,0},{16,24},{24,16},{1,9},{9,1},{17,25},{25,17},{2,10},{10... | collective-permute-start | bytes 1769480 | tf_op jit(solution)/shard_map/ppermute | solution.py:397
  135.5 15.2 %collective-permute-start.31 = (bf16[72,4096]{1,0:T(8,128)(2,1)S(1)}, bf16[72,4096]{1,0:T(8,128)(2,1)S(1)}, u32[]{:S(2)}, u32[]{:S(2)}) collective-permute-start(bf16[72,4096]{1,0:T(8,128)(2,1)S(1)} %collective-permute-done.27.refs_10_), channel_id=1, source_target_pairs={{0,8},{8,0},{16,24},{24,16},{1,9},{9,1},{17,25},{25,17},{2,10},{10... | collective-permute-start | bytes 1769480 | tf_op jit(solution)/shard_map/ppermute | solution.py:397
  141.8 8.9 %collective-permute-start.21 = (bf16[48,4096]{1,0:T(8,128)(2,1)S(1)}, bf16[48,4096]{1,0:T(8,128)(2,1)S(1)}, u32[]{:S(2)}, u32[]{:S(2)}) collective-permute-start(bf16[48,4096]{1,0:T(8,128)(2,1)S(1)} %join_rows.3.refs_0_), channel_id=1, source_target_pairs={{0,8},{8,0},{16,24},{24,16},{1,9},{9,1},{17,25},{25,17},{2,10},{10... | collective-permute-start | bytes 1179656 | tf_op jit(solution)/shard_map/ppermute | solution.py:397
  141.8 8.9 %collective-permute-start.32 = (bf16[48,4096]{1,0:T(8,128)(2,1)S(1)}, bf16[48,4096]{1,0:T(8,128)(2,1)S(1)}, u32[]{:S(2)}, u32[]{:S(2)}) collective-permute-start(bf16[48,4096]{1,0:T(8,128)(2,1)S(1)} %collective-permute-done.28.refs_11_), channel_id=1, source_target_pairs={{0,8},{8,0},{16,24},{24,16},{1,9},{9,1},{17,25},{25,17},{2,10},{10... | collective-permute-start | bytes 1179656 | tf_op jit(solution)/shard_map/ppermute | solution.py:397
  148.9 1.8 %collective-permute-start.29 = (bf16[48,4096]{1,0:T(8,128)(2,1)S(1)}, bf16[48,4096]{1,0:T(8,128)(2,1)S(1)}, u32[]{:S(2)}, u32[]{:S(2)}) collective-permute-start(bf16[48,4096]{1,0:T(8,128)(2,1)S(1)} %collective-permute-done.25.refs_8_), channel_id=1, source_target_pairs={{0,8},{8,0},{16,24},{24,16},{1,9},{9,1},{17,25},{25,17},{2,10},{10... | collective-permute-start | bytes 1179656 | tf_op jit(solution)/shard_map/ppermute | solution.py:397
